TPU v7x, 32 devices: a whole 2x2x4 slice. The times are simulated.
32 devices in a mesh: wide: 8 (over z, x), narrow: 4 (over y, core).
Axes of the slice: x: 2, y: 2, z: 4, core: 2. Of those that a mesh axis runs over, the one named last changes fastest.
Arguments:
- layer_in: bfloat16 [16, 1024, 768], P('wide', 'narrow'), may hold values from -6 to 6
- doc_ids: int32 [16, 1024], P('wide'), may hold values from 0 to 3, never falling along the last dimension, each value on 1 to 512 neighbouring positions
- in_proj: bfloat16 [3, 768, 768], P(None, ('wide', 'narrow')), may hold values from -0.21875 to 0.21875
- out_proj: bfloat16 [768, 768], P(('wide', 'narrow')), may hold values from -1.75 to 1.75
- vec_bias: bfloat16 [6, 768], P(None, ('wide', 'narrow')), may hold values from -3 to 3
- norm_gain: bfloat16 [2, 768], P(None, ('wide', 'narrow')), may hold values from 0.5 to 1.5
- ffn_in: bfloat16 [768, 3072], P(('wide', 'narrow')), may hold values from -0.21875 to 0.21875
- ffn_bias: bfloat16 [3072], P(('wide', 'narrow')), may hold values from -3 to 3
- ffn_out: bfloat16 [3072, 768], P(('wide', 'narrow')), may hold values from -0.109375 to 0.109375
- out_grad: bfloat16 [16, 1024, 768], P('wide', 'narrow'), may hold values from -6 to 6
Outputs:
- layer_out: bfloat16 [16, 1024, 768], P('wide', 'narrow')
- grad_in: bfloat16 [16, 1024, 768], P('wide', 'narrow')
- grad_in_proj: float32 [3, 768, 768], P(None, ('wide', 'narrow'))
- grad_out_proj: float32 [768, 768], P(('wide', 'narrow'))
- grad_vec_bias: float32 [6, 768], P(None, ('wide', 'narrow'))
- grad_norm_gain: float32 [2, 768], P(None, ('wide', 'narrow'))
- grad_ffn_in: float32 [768, 3072], P(('wide', 'narrow'))
- grad_ffn_bias: float32 [3072], P(('wide', 'narrow'))
- grad_ffn_out: float32 [3072, 768], P(('wide', 'narrow'))
Inputs may be any that keep to these rules, and one draw needn't show every extreme that they name: `doc_ids`: documents are packed end to end in each slot. Along the positions of a slot the ids never fall; each of the 4 ids holds 1 to 512 consecutive positions, one of them exactly 512.
All inputs are finite; a program needn't handle non-finite values.
Results may differ from a plain program's by a relative error of at most 0.015.
Values may be sent and summed in bfloat16 or wider, within the bound.
No kernel may reach another device: no remote copies, remote signals or barrier semaphores. Data moves between devices by JAX's collectives and lax.ppermute only.
A program may use at most 192 MiB of HBM per device.

v0:
```python
import jax
import jax.numpy as jnp
from jax import lax
from jax.sharding import PartitionSpec as P

HEADS = 12
DH = 64
D = 768


eps = 1e-05


def layer_norm(rows_in, scale_vec, shift_vec):
    average = jnp.mean(rows_in, -1, keepdims=True)
    centered = rows_in - average
    variance = jnp.mean(centered * centered, -1, keepdims=True)
    return centered * lax.rsqrt(variance + eps) * scale_vec + shift_vec


def gelu_exact(upper):
    return 0.5 * upper * (1.0 + lax.erf(upper * 0.7071067811865476))


def matmul(left, right):
    return jnp.dot(left, right, preferred_element_type=jnp.float32)


def times_transposed(left, right):
    return lax.dot_general(
        left, right, (((1,), (1,)), ((), ())), preferred_element_type=jnp.float32
    )


def left_inner(left, right):
    return lax.dot_general(
        left, right, (((0,), (0,)), ((), ())), preferred_element_type=jnp.float32
    )


def project(tokens, in_full, bias_full):
    queries = ((matmul(tokens, in_full[0]) + bias_full[0]) * 0.125).astype(jnp.bfloat16)
    key_rows = matmul(tokens, in_full[1]).astype(jnp.bfloat16)
    value_rows = (matmul(tokens, in_full[2]) + bias_full[1]).astype(jnp.bfloat16)
    return (queries, key_rows, value_rows)


def heads_of(rows):
    return rows.reshape(rows.shape[0], HEADS, DH)


def slot_scores(queries, key_rows, ids_query, ids_key):
    scores = jnp.einsum(
        "qhd,khd->hqk", heads_of(queries), heads_of(key_rows), preferred_element_type=jnp.float32
    )
    allowed = ids_query[:, None] == ids_key[None, :]
    return jnp.where(allowed[None], scores, -1000000000.0)


def attend(block_items):
    queries, key_rows, value_rows, ids_query, ids_key = block_items
    scores = slot_scores(queries, key_rows, ids_query, ids_key)
    row_top = jnp.max(scores, -1, keepdims=True)
    exp_scores = jnp.exp(scores - row_top)
    row_total = jnp.sum(exp_scores, -1, keepdims=True)
    probs_low = (exp_scores / row_total).astype(jnp.bfloat16)
    mixed_rows = jnp.einsum(
        "hqk,khd->qhd", probs_low, heads_of(value_rows), preferred_element_type=jnp.float32
    )
    log_total = (row_top + jnp.log(row_total))[..., 0]
    return (mixed_rows.reshape(queries.shape[0], D).astype(jnp.bfloat16), log_total)


def attend_back(block_items):
    queries, key_rows, value_rows, ids_query, ids_key, log_total, grad_mixed = block_items
    scores = slot_scores(queries, key_rows, ids_query, ids_key)
    attn_probs = jnp.exp(scores - log_total[..., None])
    heads_g = heads_of(grad_mixed)
    grad_probs = jnp.einsum(
        "qhd,khd->hqk", heads_g, heads_of(value_rows), preferred_element_type=jnp.float32
    )
    row_inner = jnp.sum(attn_probs * grad_probs, -1, keepdims=True)
    grad_scores = (attn_probs * (grad_probs - row_inner)).astype(jnp.bfloat16)
    grad_queries = jnp.einsum(
        "hqk,khd->qhd", grad_scores, heads_of(key_rows), preferred_element_type=jnp.float32
    )
    grad_keys = jnp.einsum(
        "hqk,qhd->khd", grad_scores, heads_of(queries), preferred_element_type=jnp.float32
    )
    grad_values = jnp.einsum(
        "hqk,qhd->khd", attn_probs.astype(jnp.bfloat16), heads_g, preferred_element_type=jnp.float32
    )
    return (
        grad_queries.reshape(queries.shape[0], D),
        grad_keys.reshape(key_rows.shape[0], D),
        grad_values.reshape(value_rows.shape[0], D),
    )


def tail_forward(tokens, mixed_flat, out_full, ffn_full, bias_full, gain_full):
    weight_in, bias_in, weight_out = ffn_full
    first_sum = tokens.astype(jnp.float32) + matmul(mixed_flat, out_full) + bias_full[2]
    normed = layer_norm(
        first_sum, gain_full[0].astype(jnp.float32), bias_full[3].astype(jnp.float32)
    )
    normed_low = normed.astype(jnp.bfloat16)
    upper = matmul(normed_low, weight_in) + bias_in
    active = gelu_exact(upper).astype(jnp.bfloat16)
    second_sum = normed + matmul(active, weight_out) + bias_full[4]
    result = layer_norm(
        second_sum, gain_full[1].astype(jnp.float32), bias_full[5].astype(jnp.float32)
    )
    return (first_sum, normed_low, upper, active, second_sum, result)


def local(
    layer_in, doc_ids, in_proj, out_proj, vec_bias, norm_gain, ffn_in, ffn_bias, ffn_out, out_grad
):
    slot_count, shard_rows, model_width = layer_in.shape
    offset = lax.axis_index("narrow") * shard_rows
    ids_local = lax.dynamic_slice_in_dim(doc_ids, offset, shard_rows, 1)
    tokens = layer_in.reshape(slot_count * shard_rows, model_width)
    in_full, out_full, bias_full, gain_full = (
        lax.all_gather(in_proj, ("wide", "narrow"), axis=1, tiled=True),
        lax.all_gather(out_proj, ("wide", "narrow"), axis=0, tiled=True),
        lax.all_gather(vec_bias, ("wide", "narrow"), axis=1, tiled=True),
        lax.all_gather(norm_gain, ("wide", "narrow"), axis=1, tiled=True),
    )
    queries, key_rows, value_rows = project(tokens, in_full, bias_full)
    keys_all, values_all = (
        lax.all_gather(
            key_rows.reshape(slot_count, shard_rows, model_width), "narrow", axis=1, tiled=True
        ),
        lax.all_gather(
            value_rows.reshape(slot_count, shard_rows, model_width), "narrow", axis=1, tiled=True
        ),
    )
    queries_slot = queries.reshape(slot_count, shard_rows, model_width)
    mixed_rows, log_total = lax.map(
        attend, (queries_slot, keys_all, values_all, ids_local, doc_ids)
    )
    mixed_flat = mixed_rows.reshape(-1, model_width)
    ffn_full = (
        lax.all_gather(ffn_in, ("wide", "narrow"), axis=0, tiled=True),
        lax.all_gather(ffn_bias, ("wide", "narrow"), axis=0, tiled=True),
        lax.all_gather(ffn_out, ("wide", "narrow"), axis=0, tiled=True),
    )
    first_sum, normed_low, upper, active, second_sum, result = tail_forward(
        tokens, mixed_flat, out_full, ffn_full, bias_full, gain_full
    )
    layer_out = result.reshape(slot_count, shard_rows, model_width).astype(jnp.bfloat16)
    in_full, out_full, bias_full, gain_full = (
        lax.all_gather(in_proj, ("wide", "narrow"), axis=1, tiled=True),
        lax.all_gather(out_proj, ("wide", "narrow"), axis=0, tiled=True),
        lax.all_gather(vec_bias, ("wide", "narrow"), axis=1, tiled=True),
        lax.all_gather(norm_gain, ("wide", "narrow"), axis=1, tiled=True),
    )
    queries, key_rows, value_rows = project(tokens, in_full, bias_full)
    keys_all, values_all = (
        lax.all_gather(
            key_rows.reshape(slot_count, shard_rows, model_width), "narrow", axis=1, tiled=True
        ),
        lax.all_gather(
            value_rows.reshape(slot_count, shard_rows, model_width), "narrow", axis=1, tiled=True
        ),
    )
    queries_slot = queries.reshape(slot_count, shard_rows, model_width)
    mixed_rows, log_total = lax.map(
        attend, (queries_slot, keys_all, values_all, ids_local, doc_ids)
    )
    mixed_flat = mixed_rows.reshape(-1, model_width)
    ffn_full = (
        lax.all_gather(ffn_in, ("wide", "narrow"), axis=0, tiled=True),
        lax.all_gather(ffn_bias, ("wide", "narrow"), axis=0, tiled=True),
        lax.all_gather(ffn_out, ("wide", "narrow"), axis=0, tiled=True),
    )
    first_sum, normed_low, upper, active, second_sum, result = tail_forward(
        tokens, mixed_flat, out_full, ffn_full, bias_full, gain_full
    )
    weight_in, bias_in, weight_out = ffn_full
    grad_out = out_grad.reshape(-1, model_width).astype(jnp.float32)
    second_pull = jax.vjp(
        layer_norm, second_sum, gain_full[1].astype(jnp.float32), bias_full[5].astype(jnp.float32)
    )[1]
    grad_second, grad_gain_two, grad_shift_two = second_pull(grad_out)
    grad_down = grad_second.astype(jnp.bfloat16)
    grad_weight_out = left_inner(active, grad_down)
    grad_bias_down = jnp.sum(grad_down.astype(jnp.float32), 0)
    grad_active = times_transposed(grad_down, weight_out)
    gelu_pull = jax.vjp(gelu_exact, upper)[1]
    grad_upper = gelu_pull(grad_active)[0].astype(jnp.bfloat16)
    grad_weight_in = left_inner(normed_low, grad_upper)
    grad_bias_in = jnp.sum(grad_upper.astype(jnp.float32), 0)
    grad_normed = grad_second + times_transposed(grad_upper, weight_in)
    first_pull = jax.vjp(
        layer_norm, first_sum, gain_full[0].astype(jnp.float32), bias_full[3].astype(jnp.float32)
    )[1]
    grad_first, grad_gain_one, grad_shift_one = first_pull(grad_normed)
    grad_attn = grad_first.astype(jnp.bfloat16)
    grad_weight_o = left_inner(mixed_flat, grad_attn)
    grad_bias_o = jnp.sum(grad_attn.astype(jnp.float32), 0)
    grad_mixed = times_transposed(grad_attn, out_full).astype(jnp.bfloat16)
    grad_mixed_slot = grad_mixed.reshape(slot_count, shard_rows, model_width)
    back_parts = lax.map(
        attend_back,
        (queries_slot, keys_all, values_all, ids_local, doc_ids, log_total, grad_mixed_slot),
    )
    grad_query_rows, grad_keys_all, grad_values_all = back_parts
    grad_keys, grad_values = (
        lax.psum_scatter(
            grad_keys_all.astype(jnp.bfloat16), "narrow", scatter_dimension=1, tiled=True
        ).astype(jnp.float32),
        lax.psum_scatter(
            grad_values_all.astype(jnp.bfloat16), "narrow", scatter_dimension=1, tiled=True
        ).astype(jnp.float32),
    )
    grad_keys = grad_keys.reshape(-1, model_width).astype(jnp.bfloat16)
    grad_values = grad_values.reshape(-1, model_width).astype(jnp.bfloat16)
    grad_queries = grad_query_rows.reshape(-1, model_width).astype(jnp.bfloat16) * 0.125
    grad_tokens = (
        grad_first
        + times_transposed(grad_queries, in_full[0])
        + times_transposed(grad_keys, in_full[1])
        + times_transposed(grad_values, in_full[2])
    )
    grad_proj_stack = jnp.stack(
        [
            left_inner(tokens, grad_queries),
            left_inner(tokens, grad_keys),
            left_inner(tokens, grad_values),
        ]
    )
    grad_bias_q = jnp.sum(grad_queries.astype(jnp.float32), 0)
    grad_bias_v = jnp.sum(grad_values.astype(jnp.float32), 0)
    grad_bias_stack = jnp.stack(
        [grad_bias_q, grad_bias_v, grad_bias_o, grad_shift_one, grad_bias_down, grad_shift_two]
    )
    grad_gain_stack = jnp.stack([grad_gain_one, grad_gain_two])
    grad_in_proj, grad_out_proj, grad_vec_bias, grad_norm_gain = (
        lax.psum_scatter(grad_proj_stack, ("wide", "narrow"), scatter_dimension=1, tiled=True),
        lax.psum_scatter(grad_weight_o, ("wide", "narrow"), scatter_dimension=0, tiled=True),
        lax.psum_scatter(grad_bias_stack, ("wide", "narrow"), scatter_dimension=1, tiled=True),
        lax.psum_scatter(grad_gain_stack, ("wide", "narrow"), scatter_dimension=1, tiled=True),
    )
    grad_ffn_in, grad_ffn_bias, grad_ffn_out = (
        lax.psum_scatter(grad_weight_in, ("wide", "narrow"), scatter_dimension=0, tiled=True),
        lax.psum_scatter(grad_bias_in, ("wide", "narrow"), scatter_dimension=0, tiled=True),
        lax.psum_scatter(grad_weight_out, ("wide", "narrow"), scatter_dimension=0, tiled=True),
    )
    grad_in = grad_tokens.reshape(slot_count, shard_rows, model_width).astype(jnp.bfloat16)
    return (
        layer_out,
        grad_in,
        grad_in_proj,
        grad_out_proj,
        grad_vec_bias,
        grad_norm_gain,
        grad_ffn_in,
        grad_ffn_bias,
        grad_ffn_out,
    )


def solution(mesh):
    return jax.shard_map(
        local,
        mesh=mesh,
        in_specs=(
            P("wide", "narrow", None),
            P("wide", None),
            P(None, ("wide", "narrow"), None),
            P(("wide", "narrow"), None),
            P(None, ("wide", "narrow")),
            P(None, ("wide", "narrow")),
            P(("wide", "narrow"), None),
            P(("wide", "narrow")),
            P(("wide", "narrow"), None),
            P("wide", "narrow", None),
        ),
        out_specs=(
            P("wide", "narrow", None),
            P("wide", "narrow", None),
            P(None, ("wide", "narrow"), None),
            P(("wide", "narrow"), None),
            P(None, ("wide", "narrow")),
            P(None, ("wide", "narrow")),
            P(("wide", "narrow"), None),
            P(("wide", "narrow")),
            P(("wide", "narrow"), None),
        ),
        check_vma=False,
    )
```

profile of v0, /device:TPU:0, one launch (start us, length us, event | category | flops | bytes accessed | tf_op | source)
XLA Modules:
  0.0 1177.1 jit_solution(18239429949410236350)
XLA Ops:
  8.0 43.8 %all-gather = bf16[32,24,6]{1,2,0:T(8,128)(2,1)S(1)} all-gather(bf16[1,24,6]{1,2,0:T(8,128)(2,1)} %bitcast.277), channel_id=1, replica_groups=mesh['wide'=8,'narrow'=4] {'wide','narrow'}, dimensions={0}, use_global_device_ids=true | all-gather | bytes 9504 | tf_op jit(solution)/shard_map/all_gather | solution.py:126
  52.5 21.1 %all-gather.9.cloned.1.call-done = bf16[3,768,768]{2,1,0:T(8,128)(2,1)} async-done(((bf16[3,24,768]{2,1,0:T(8,128)(2,1)}), bf16[3,768,768]{2,1,0:T(8,128)(2,1)}) %all-gather.9.cloned.1.call-update) | async-done | bytes 3538960 | tf_op jit(solution)/shard_map/all_gather | solution.py:124
  73.6 2.3 add_convert_fusion.3
  77.1 2.1 convolution_convert_fusion.1
  82.3 39.4 %all-gather.1 = bf16[32,24,2]{1,2,0:T(2,128)(2,1)S(1)} all-gather(bf16[1,24,2]{1,2,0:T(2,128)(2,1)S(1)} %bitcast.278), channel_id=1, replica_groups=mesh['wide'=8,'narrow'=4] {'wide','narrow'}, dimensions={0}, use_global_device_ids=true | all-gather | bytes 3168 | tf_op jit(solution)/shard_map/all_gather | solution.py:127
  122.0 37.3 %all-reduce = bf16[3072]{0:T(1024)(128)(2,1)S(1)} all-reduce(bf16[3072]{0:T(1024)(128)(2,1)S(1)} %dynamic-update-slice), channel_id=1, replica_groups=mesh['wide'=8,'narrow'=4] {'wide','narrow'}, use_global_device_ids=true, to_apply=%add | all-reduce | flops 3072 | bytes 12288
  160.6 2.1 multiply_convert_fusion.3
  163.9 46.1 %while.36 = (s32[]{:T(128)}, bf16[2,256,768]{2,1,0:T(8,128)(2,1)}, bf16[2,1024,768]{1,2,0:T(8,128)(2,1)}, s32[2,256]{1,0:T(2,128)S(1)}, s32[2,1024]{1,0:T(2,128)...) while((s32[]{:T(128)}, bf16[2,256,768]{2,1,0:T(8,128)(2,1)}, ...), condition=%wide.region_3.4_spmd, body=%wide.region_0.3_spmd.sunk | while | flops 821494784 | bytes 38313572 | solution.py:139
  164.8 3.4 constant_dynamic-slice_fusion.34
  168.2 10.7 fusion.149
  178.9 6.8 fusion.150
  187.7 3.4 constant_dynamic-slice_fusion.34
  191.1 10.7 fusion.149
  201.8 6.8 fusion.150
  210.0 2.4 fusion.64
  212.7 46.1 %all-gather.17.cloned.1.call-done = bf16[768,3072]{1,0:T(8,128)(2,1)} async-done(((bf16[24,3072]{1,0:T(8,128)(2,1)}), bf16[768,3072]{1,0:T(8,128)(2,1)}) %all-gather.17.cloned.1.call-update) | async-done | bytes 4718608 | tf_op jit(solution)/shard_map/all_gather | solution.py:144
  258.9 64.7 %all-gather.19.cloned.1.call-done = bf16[3072,768]{1,0:T(8,128)(2,1)} async-done(((bf16[96,768]{1,0:T(8,128)(2,1)}), bf16[3072,768]{1,0:T(8,128)(2,1)}) %all-gather.19.cloned.1.call-update) | async-done | bytes 4718608 | tf_op jit(solution)/shard_map/all_gather | solution.py:146
  323.5 10.3 fusion.65
  333.9 25.2 %while.37 = (s32[]{:T(128)}, bf16[2,256,768]{2,1,0:T(8,128)(2,1)S(1)}, f32[2,12,256]{2,1,0:T(8,128)}, bf16[2,1024,768]{1,2,0:T(8,128)(2,1)}, s32[2,256]{1,0:T(2,...) while((s32[]{:T(128)}, ...), condition=%wide.region_11.12_spmd, body=%wide.region_8.11_spmd.sunk | while | flops 834073600 | bytes 51498608 | solution.py:168
  334.2 2.2 constant_dynamic-slice_fusion.38
  336.4 2.1 select_reduce_fusion.3
  338.5 3.4 fusion.154
  342.5 3.7 fusion.155
  346.7 2.2 constant_dynamic-slice_fusion.38
  348.9 2.1 select_reduce_fusion.3
  351.0 3.4 fusion.154
  355.0 3.7 fusion.155
  359.1 2.4 fusion.62
  362.1 3.3 multiply_convert_fusion.1
  365.5 2.8 fusion.63
  373.9 5.9 convert_reduce_fusion
  379.8 3.7 multiply_reduce_fusion.1
  388.0 107.5 %while.38 = (s32[]{:T(128)}, bf16[2,256,768]{2,1,0:T(8,128)(2,1)}, bf16[2,1024,768]{2,1,0:T(8,128)(2,1)}, bf16[2,1024,768]{2,1,0:T(8,128)(2,1)}, bf16[2,1024,768...) while((s32[]{:T(128)}, bf16[2,256,768]{2,1,0:T(8,128)(2,1)}, ...), condition=%wide.region_22.23_spmd, body=%wide.region_20.22_spmd.sunk | while | flops 2051273728 | bytes 242012336 | solution.py:204
  390.3 6.3 fusion.166
  399.6 11.4 multiply_reduce_fusion.8
  412.2 6.5 multiply_convert_fusion.5
  422.9 8.7 fusion.168
  431.6 2.7 copy.110
  434.3 3.5 constant_dynamic-update-slice_fusion.12
  438.7 2.0 fusion.167
  443.8 6.3 fusion.166
  453.2 11.4 multiply_reduce_fusion.8
  465.7 6.5 multiply_convert_fusion.5
  476.4 8.7 fusion.168
  485.2 2.7 copy.110
  487.9 3.4 constant_dynamic-update-slice_fusion.12
  492.3 2.0 fusion.167
  498.6 33.3 %reduce-scatter.10.cloned.1.call-done = bf16[2,256,768]{2,1,0:T(8,128)(2,1)} async-done(((bf16[2,1024,768]{2,1,0:T(8,128)(2,1)}), bf16[2,256,768]{2,1,0:T(8,128)(2,1)}) %reduce-scatter.10.cloned.1.call-update) | async-done | bytes 786448 | tf_op jit(solution)/shard_map/reduce_scatter | solution.py:213
  531.8 3.4 convolution_bitcast_fusion
  535.2 37.1 %reduce-scatter.8.cloned.1.call-done = bf16[2,256,768]{2,1,0:T(8,128)(2,1)} async-done(((bf16[2,1024,768]{2,1,0:T(8,128)(2,1)}), bf16[2,256,768]{2,1,0:T(8,128)(2,1)}) %reduce-scatter.8.cloned.1.call-update) | async-done | bytes 786448 | tf_op jit(solution)/shard_map/reduce_scatter | solution.py:210
  572.3 2.1 convolution_bitcast_fusion.1
  574.4 3.3 pad_maximum_fusion
  577.7 11.0 copy.59
  590.0 2.2 fusion.71
  593.7 8.1 fusion.55
  603.0 8.3 fusion.72
  612.8 3.4 fusion.30
  616.4 40.8 %all-reduce.5 = (f32[6,768]{1,0:T(8,128)S(1)}, f32[2,768]{1,0:T(2,128)S(1)}, f32[3072]{0:T(1024)S(1)}) all-reduce(f32[6,768]{1,0:T(8,128)S(1)} %stack.42, f32[2,768]{1,0:T(2,128)S(1)} %pad_maximum_fusion.1, f32[3072]{0:T(1024)S(1)} %copy-done.51), channel_id=6, replica_groups=mesh['wide'=8,'narrow'=4] {'wide','narrow'}, use_global_device_ids=true, to_apply=%region_33.34.clone | all-reduce | flops 9216 | bytes 73728
  659.1 2.3 fusion.31
  661.4 3.0 add_convert_fusion.1
  664.4 116.8 %all-reduce.8.cloned.1.call-done = f32[3,768,768]{2,0,1:T(4,128)} async-done(((f32[3,768,768]{2,0,1:T(4,128)}), f32[3,768,768]{2,0,1:T(4,128)}) %all-reduce.8.cloned.1.call-update) | async-done | bytes 7077904
  782.9 103.6 %reduce-scatter.12.cloned.1.call-done = f32[24,768]{1,0:T(8,128)} async-done(((f32[768,768]{1,0:T(8,128)}), f32[24,768]{1,0:T(8,128)}) %reduce-scatter.12.cloned.1.call-update) | async-done | bytes 73744 | tf_op jit(solution)/shard_map/reduce_scatter | solution.py:241
  886.5 142.0 %reduce-scatter.14.cloned.1.call-done = f32[24,3072]{1,0:T(8,128)} async-done(((f32[768,3072]{1,0:T(8,128)}), f32[24,3072]{1,0:T(8,128)}) %reduce-scatter.14.cloned.1.call-update) | async-done | bytes 294928 | tf_op jit(solution)/shard_map/reduce_scatter | solution.py:246
  1028.6 141.5 %reduce-scatter.16.cloned.1.call-done = f32[96,768]{1,0:T(8,128)} async-done(((f32[3072,768]{1,0:T(8,128)}), f32[96,768]{1,0:T(8,128)}) %reduce-scatter.16.cloned.1.call-update) | async-done | bytes 294928 | tf_op jit(solution)/shard_map/reduce_scatter | solution.py:248
  (319 shorter events, 61.7 us)
Async XLA Ops:
  7.2 66.4 %all-gather.9.cloned.1.call-start = ((), (), s32[]{:S(2)}) async-start(), calls=%async_computation.5 | async-start | bytes 3649536 | tf_op jit(solution)/shard_map/all_gather | solution.py:124
  7.9 155.0 %all-gather.11.cloned.1.call-start = ((), (), s32[]{:S(2)}) async-start(), calls=%async_computation.6 | async-start | bytes 3932160 | tf_op jit(solution)/shard_map/all_gather | solution.py:134
  77.1 85.9 %all-gather.13.cloned.1.call-start = ((), (), s32[]{:S(2)}) async-start(), calls=%async_computation.7 | async-start | bytes 3932160 | tf_op jit(solution)/shard_map/all_gather | solution.py:131
  79.2 3.1 copy-start.60
  79.2 42.6 %copy-start.63 = (bf16[96]{0:T(256)(128)(2,1)S(1)}, bf16[96]{0:T(256)(128)(2,1)}, u32[]{:S(2)}) copy-start(bf16[96]{0:T(256)(128)(2,1)} %param.23) | copy-start | bytes 580
  79.2 80.7 %copy-start.34 = (s32[2,1024]{1,0:T(2,128)S(1)}, s32[2,1024]{1,0:T(2,128)}, u32[]{:S(2)}) copy-start(s32[2,1024]{1,0:T(2,128)} %param.17) | copy-start | bytes 24580
  80.4 129.6 %all-gather.15.cloned.1.call-start = ((), (), s32[]{:S(2)}) async-start(), calls=%async_computation.8 | async-start | bytes 1216512 | tf_op jit(solution)/shard_map/all_gather | solution.py:125
  81.0 177.9 %all-gather.17.cloned.1.call-start = ((), (), s32[]{:S(2)}) async-start(), calls=%async_computation.9 | async-start | bytes 4866048 | tf_op jit(solution)/shard_map/all_gather | solution.py:144
  81.6 241.9 %all-gather.19.cloned.1.call-start = ((), (), s32[]{:S(2)}) async-start(), calls=%async_computation.10 | async-start | bytes 4866048 | tf_op jit(solution)/shard_map/all_gather | solution.py:146
  82.1 449.7 %reduce-scatter.10.cloned.1.call-start = ((), (), s32[]{:S(2)}) async-start(), calls=%async_computation.12 | async-start | bytes 3932160 | tf_op jit(solution)/shard_map/reduce_scatter | solution.py:213
  160.6 223.0 %copy-start.47 = (f32[768]{0:T(1024)}, f32[768]{0:T(1024)S(1)}, u32[]{:S(2)}) copy-start(f32[768]{0:T(1024)S(1)} %get-tuple-element.271) | copy-start | bytes 9220
  212.4 111.1 %copy-start.50 = (f32[3072]{0:T(1024)S(1)}, f32[3072]{0:T(1024)}, u32[]{:S(2)}) copy-start(f32[3072]{0:T(1024)} %convert_element_type.180) | copy-start | bytes 36868
  212.4 111.1 %copy-start.56 = (f32[768]{0:T(1024)S(1)}, f32[768]{0:T(1024)}, u32[]{:S(2)}) copy-start(f32[768]{0:T(1024)} %get-tuple-element.266) | copy-start | bytes 9220
  212.4 111.1 %copy-start.58 = (f32[768]{0:T(1024)S(1)}, f32[768]{0:T(1024)}, u32[]{:S(2)}) copy-start(f32[768]{0:T(1024)} %get-tuple-element.265) | copy-start | bytes 9220
  333.9 25.2 %copy-start.15 = (bf16[2,256,768]{2,1,0:T(8,128)(2,1)S(1)}, bf16[2,256,768]{2,1,0:T(8,128)(2,1)}, u32[]{:S(2)}) copy-start(bf16[2,256,768]{2,1,0:T(8,128)(2,1)} %param.16) | copy-start | bytes 2359300
  333.9 25.2 %copy-start.59 = (f32[768]{0:T(1024)S(1)}, f32[768]{0:T(1024)}, u32[]{:S(2)}) copy-start(f32[768]{0:T(1024)} %get-tuple-element.267) | copy-start | bytes 9220
  359.1 2.5 copy-start.22
  359.1 3.0 copy-start.61
  359.1 6.3 slice-start.3
  361.6 21.9 %copy-start.17 = (f32[512,768]{1,0:T(8,128)}, f32[512,768]{1,0:T(8,128)S(1)}, u32[]{:S(2)}) copy-start(f32[512,768]{1,0:T(8,128)S(1)} %get-tuple-element.353) | copy-start | bytes 4718596
  361.6 21.9 %copy-start.40 = (f32[512]{0:T(512)}, f32[512]{0:T(512)S(1)}, u32[]{:S(2)}) copy-start(f32[512]{0:T(512)S(1)} %broadcast_multiply_fusion.1) | copy-start | bytes 6148
  362.1 21.4 %copy-start.52 = (f32[512]{0:T(512)}, f32[512]{0:T(512)S(1)}, u32[]{:S(2)}) copy-start(f32[512]{0:T(512)S(1)} %fusion.50) | copy-start | bytes 6148
  362.1 3.4 slice-start.4
  365.4 2.8 copy-start.64
  373.9 5.9 copy-start.32
  379.8 3.7 copy-start.65
  384.2 3.8 copy-start.9
  384.2 2.1 copy-start.62
  384.2 3.7 copy-start.42
  385.0 2.9 copy-start.25
  388.4 8.2 copy-start.35
  388.4 8.2 copy-start.37
  390.3 7.4 copy-start.24
  396.9 14.1 %copy-start.3 = (pred[256,1024]{1,0:T(8,128)(4,1)}, pred[256,1024]{1,0:T(8,128)(4,1)S(1)}, u32[]{:S(2)}) copy-start(pred[256,1024]{1,0:T(8,128)(4,1)S(1)} %broadcast_compare_fusion.8) | copy-start | bytes 786436 | tf_op jit(solution)/shard_map/while
  399.6 11.4 slice-start
  399.6 11.4 slice-start.1
  399.6 12.6 %slice-start.2 = ((s8[12582912]{0:T(1024)(128)(4,1)}), s8[4194304]{0:T(1024)(128)(4,1)S(1)}, s32[]{:S(2)}) async-start(s8[12582912]{0:T(1024)(128)(4,1)} %bitcast.232), calls=%async_computation.19 | async-start | bytes 8388608 | tf_op jit(solution)/shard_map/while
  418.7 2.6 copy-start
  431.6 2.7 copy-start.2
  434.3 4.4 copy-start.1
  438.7 2.2 copy-start.29
  441.9 8.3 copy-start.35
  441.9 8.3 copy-start.37
  443.8 7.4 copy-start.24
  450.4 14.1 %copy-start.3 = (pred[256,1024]{1,0:T(8,128)(4,1)}, pred[256,1024]{1,0:T(8,128)(4,1)S(1)}, u32[]{:S(2)}) copy-start(pred[256,1024]{1,0:T(8,128)(4,1)S(1)} %broadcast_compare_fusion.8) | copy-start | bytes 786436 | tf_op jit(solution)/shard_map/while
  453.1 11.4 slice-start
  453.1 11.4 slice-start.1
  453.1 12.6 %slice-start.2 = ((s8[12582912]{0:T(1024)(128)(4,1)}), s8[4194304]{0:T(1024)(128)(4,1)S(1)}, s32[]{:S(2)}) async-start(s8[12582912]{0:T(1024)(128)(4,1)} %bitcast.232), calls=%async_computation.19 | async-start | bytes 8388608 | tf_op jit(solution)/shard_map/while
  472.3 2.6 copy-start
  485.2 2.7 copy-start.2
  487.9 4.4 copy-start.1
  492.3 2.2 copy-start.29
  495.5 76.8 %reduce-scatter.8.cloned.1.call-start = ((), (), s32[]{:S(2)}) async-start(), calls=%async_computation.11 | async-start | bytes 3932160 | tf_op jit(solution)/shard_map/reduce_scatter | solution.py:210
  496.2 284.9 %all-reduce.8.cloned.1.call-start = ((), (), s32[]{:S(2)}) async-start(), calls=%async_computation.16 | async-start | bytes 18874368
  572.3 2.1 copy-start.8
  588.7 297.8 %reduce-scatter.12.cloned.1.call-start = ((), (), s32[]{:S(2)}) async-start(), calls=%async_computation.13 | async-start | bytes 2433024 | tf_op jit(solution)/shard_map/reduce_scatter | solution.py:241
  592.3 436.2 %reduce-scatter.14.cloned.1.call-start = ((), (), s32[]{:S(2)}) async-start(), calls=%async_computation.14 | async-start | bytes 9732096 | tf_op jit(solution)/shard_map/reduce_scatter | solution.py:246
  601.9 568.2 %reduce-scatter.16.cloned.1.call-start = ((), (), s32[]{:S(2)}) async-start(), calls=%async_computation.15 | async-start | bytes 9732096 | tf_op jit(solution)/shard_map/reduce_scatter | solution.py:248
  612.7 3.4 copy-start.11
  612.7 3.6 copy-start.51
  612.7 46.3 %copy-start.27 = (bf16[2,256,768]{2,1,0:T(8,128)(2,1)S(1)}, bf16[2,256,768]{2,1,0:T(8,128)(2,1)}, u32[]{:S(2)}) copy-start(bf16[2,256,768]{2,1,0:T(8,128)(2,1)} %reduce-scatter.8.cloned.1.call-done) | copy-start | bytes 2359300
  659.0 2.3 copy-start.10
  659.0 2.3 copy-start.28
  659.0 2.3 copy-start.43
  (37 other events, 49.7 us)
Sparse Core Ops, SparseCore 0:
  10.8 62.7 all-gather.8
  77.2 27.7 all-gather.10
  107.2 29.5 all-gather.12
  139.5 54.0 all-gather.14
  196.3 62.4 all-gather.16
  261.6 61.8 all-gather.18
  495.6 36.1 reduce-scatter.9
  534.4 37.8 reduce-scatter.7
  588.8 192.3 all-reduce.7
  786.9 99.5 reduce-scatter.11
  893.0 135.5 reduce-scatter.13
  1034.9 135.0 reduce-scatter.15
where the time goes:
time: 1190 us; the launch traced here: 1180 us
  waiting for transfers between devices  709 us (60%)
  matrix products  178 us (15%)
  blocking collectives  161 us (14%)
  local copies, waits for them, and re-layouts  74.7 us (6%)
  other arithmetic  35.9 us (3%)
  between operations  15.2 us (1%)
    reduce_scatter x1, waiting for transfers between devices, local(): lax.psum_scatter(grad_weight_in, ('wide', 'narrow'), scatter_dimension=0,...  142 us
    reduce_scatter x1, waiting for transfers between devices, local(): lax.psum_scatter(grad_weight_out, ('wide', 'narrow'), scatter_dimension=0...  141 us
    unnamed x13, waiting for transfers between devices  120 us
    reduce_scatter x1, waiting for transfers between devices, local(): lax.psum_scatter(grad_weight_o, ('wide', 'narrow'), scatter_dimension=0,...  104 us
    unnamed x2, blocking collectives  78.1 us
    all_gather x1, waiting for transfers between devices, local(): lax.all_gather(ffn_out, ('wide', 'narrow'), axis=0, tiled=True)  64.7 us
    all_gather x1, waiting for transfers between devices, local(): lax.all_gather(ffn_in, ('wide', 'narrow'), axis=0, tiled=True)  46.1 us
    all_gather x1, blocking collectives, local(): lax.all_gather(vec_bias, ('wide', 'narrow'), axis=1, tiled=True)  43.8 us
  transfers between devices with their start and end apart: 12, of which 9 were waited for; matrix products, arithmetic and copies ran while one was open for 8% of the time, Pallas kernels for 0%

commit v1 on v0

v1 whole, which is shorter than its diff:
```python
import jax
import jax.numpy as jnp
from jax import lax
from jax.experimental import pallas as pl
from jax.experimental.pallas import tpu as pltpu
from jax.sharding import PartitionSpec as P

D = 768
FF = 3072
DH = 64
PAIR = 128
TRIO = 3 * PAIR
HALF = D // 2
QB = 256
AXES = ("wide", "narrow")
EPS = 1e-05
BF = jnp.bfloat16
F32 = jnp.float32
MASKED = -1000000000.0
SMALL = 128


def matmul(left, right):
    return jnp.dot(left, right, preferred_element_type=F32)


def times_transposed(left, right):
    return lax.dot_general(left, right, (((1,), (1,)), ((), ())), preferred_element_type=F32)


def left_inner(left, right):
    return lax.dot_general(left, right, (((0,), (0,)), ((), ())), preferred_element_type=F32)


def attend_kernel(trio_ref, id_col_ref, id_row_ref, mixed_ref, lse_ref):
    total = trio_ref.shape[0]

    def block(step, carry):
        rows = pl.ds(pl.multiple_of(step * QB, QB), QB)
        same = id_col_ref[...] == id_row_ref[:, rows]
        pieces = []
        for head in range(2):
            q = trio_ref[rows, head * DH : (head + 1) * DH]
            k = trio_ref[:, PAIR + head * DH : PAIR + (head + 1) * DH]
            v = trio_ref[:, 2 * PAIR + head * DH : 2 * PAIR + (head + 1) * DH]
            scores = jnp.where(same, times_transposed(k, q), MASKED)
            top = jnp.max(scores, 0, keepdims=True)
            weights = jnp.exp(scores - top)
            mass = jnp.sum(weights, 0, keepdims=True)
            pieces.append(left_inner(v, weights.astype(BF)) / mass)
            lse_ref[0, head : head + 1, rows] = top + jnp.log(mass)
        mixed_ref[rows, :] = jnp.concatenate(pieces, 0).T.astype(BF)
        return carry

    lax.fori_loop(0, total // QB, block, 0)


def attend(trios, id_col, id_row):
    total, width = trios.shape
    pairs = width // TRIO
    return pl.pallas_call(
        attend_kernel,
        grid=(pairs,),
        in_specs=[
            pl.BlockSpec((total, TRIO), lambda p: (0, p)),
            pl.BlockSpec((total, 1), lambda p: (0, 0)),
            pl.BlockSpec((1, total), lambda p: (0, 0)),
        ],
        out_specs=[
            pl.BlockSpec((total, PAIR), lambda p: (0, p)),
            pl.BlockSpec((1, 2, total), lambda p: (p, 0, 0)),
        ],
        out_shape=[
            jax.ShapeDtypeStruct((total, pairs * PAIR), BF),
            jax.ShapeDtypeStruct((pairs, 2, total), F32),
        ],
        cost_estimate=pl.CostEstimate(
            flops=4 * total * total * PAIR * pairs * 4,
            transcendentals=2 * pairs * total * total,
            bytes_accessed=total * width * 4,
        ),
        name="attend",
    )(trios, id_col, id_row)


def attend_back_kernel(trio_ref, grad_ref, id_col_ref, id_row_ref, lse_ref, out_ref, dk_ref, dv_ref):
    total = trio_ref.shape[0]
    dk_ref[...] = jnp.zeros_like(dk_ref)
    dv_ref[...] = jnp.zeros_like(dv_ref)

    def block(step, carry):
        rows = pl.ds(pl.multiple_of(step * QB, QB), QB)
        same = id_col_ref[...] == id_row_ref[:, rows]
        pieces = []
        for head in range(2):
            lanes = slice(head * DH, (head + 1) * DH)
            q = trio_ref[rows, lanes]
            k = trio_ref[:, PAIR + head * DH : PAIR + (head + 1) * DH]
            v = trio_ref[:, 2 * PAIR + head * DH : 2 * PAIR + (head + 1) * DH]
            g = grad_ref[rows, lanes]
            scores = times_transposed(k, q) - lse_ref[0, head : head + 1, rows]
            probs = jnp.where(same, jnp.exp(scores), 0.0)
            grad_probs = times_transposed(v, g)
            inner = jnp.sum(probs * grad_probs, 0, keepdims=True)
            grad_scores = (probs * (grad_probs - inner)).astype(BF)
            pieces.append(left_inner(k, grad_scores))
            dk_ref[:, lanes] += matmul(grad_scores, q)
            dv_ref[:, lanes] += matmul(probs.astype(BF), g)
        grad_q = jnp.concatenate(pieces, 0).T.astype(BF)
        out_ref[rows, :PAIR] = (grad_q.astype(F32) * 0.125).astype(BF)
        return carry

    lax.fori_loop(0, total // QB, block, 0)
    out_ref[:, PAIR : 2 * PAIR] = dk_ref[...].astype(BF)
    out_ref[:, 2 * PAIR :] = dv_ref[...].astype(BF)


def attend_back(trios, grads, id_col, id_row, lse):
    total, width = trios.shape
    pairs = width // TRIO
    return pl.pallas_call(
        attend_back_kernel,
        grid=(pairs,),
        in_specs=[
            pl.BlockSpec((total, TRIO), lambda p: (0, p)),
            pl.BlockSpec((total, PAIR), lambda p: (0, p)),
            pl.BlockSpec((total, 1), lambda p: (0, 0)),
            pl.BlockSpec((1, total), lambda p: (0, 0)),
            pl.BlockSpec((1, 2, total), lambda p: (p, 0, 0)),
        ],
        out_specs=pl.BlockSpec((total, TRIO), lambda p: (0, p)),
        out_shape=jax.ShapeDtypeStruct((total, width), BF),
        scratch_shapes=[pltpu.VMEM((total, PAIR), F32), pltpu.VMEM((total, PAIR), F32)],
        cost_estimate=pl.CostEstimate(
            flops=10 * total * total * PAIR * pairs * 4,
            transcendentals=2 * pairs * total * total,
            bytes_accessed=total * width * 6,
        ),
        name="attend_back",
    )(trios, grads, id_col, id_row, lse)


class Links:
    def __init__(self, mesh):
        self.devices = mesh.shape["wide"] * mesh.shape["narrow"]
        self.chips = self.devices // 2
        bits = self.chips.bit_length() - 1
        assert self.chips == 1 << bits
        self.groups = [(low, 2) for low in range(bits - 2, -1, -2)]
        if bits % 2:
            self.groups.append((0, 1))
        self.own = lax.axis_index(AXES)
        self.chip = self.own // 2
        self.core = self.own % 2

    def send(self, value, flip_even, flip_odd):
        pairs = [(d, d ^ (flip_odd if d % 2 else flip_even)) for d in range(self.devices)]
        return lax.ppermute(value, AXES, pairs)

    def core_swap(self, value):
        return self.send(value, 1, 1)

    def row_swap(self, value):
        return self.send(value, 2, 2)

    def gather(self, block):
        have = block[None]
        for low, size in self.groups:
            place = (self.chip >> low) % (1 << size)
            width = 1 << size
            full = jnp.zeros((have.shape[0], width) + block.shape, block.dtype)

            def put(full, piece, at):
                return lax.dynamic_update_slice_in_dim(full, piece[:, None], at, 1)

            full = put(full, have, place)
            if size == 1:
                full = put(full, self.send(have, 2 << low, 2 << low), place ^ 1)
            else:
                first, second = 1 + self.core, 2 - self.core
                one = self.send(have, 2 << low, 4 << low)
                two = self.send(jnp.stack([have, one]), 4 << low, 2 << low)
                full = put(full, one, place ^ first)
                full = put(full, two[0], place ^ second)
                full = put(full, two[1], place ^ 3)
            have = full.reshape((-1,) + block.shape)
        return have

    def scatter_sum(self, blocks):
        have = blocks
        for low, size in reversed(self.groups):
            place = (self.chip >> low) % (1 << size)
            width = 1 << size
            parts = have.reshape((-1, width) + blocks.shape[1:])

            def take(at):
                return lax.dynamic_index_in_dim(parts, at, 1, keepdims=False)

            if size == 1:
                got = self.send(take(place ^ 1).astype(BF), 2 << low, 2 << low)
                have = take(place).astype(F32) + got.astype(F32)
            else:
                first, second = 1 + self.core, 2 - self.core
                two = jnp.stack([take(place ^ second), take(place ^ 3)]).astype(BF)
                two = self.send(two, 4 << low, 2 << low)
                one = take(place ^ first).astype(F32) + two[1].astype(F32)
                one = self.send(one.astype(BF), 2 << low, 4 << low)
                have = take(place).astype(F32) + two[0].astype(F32) + one.astype(F32)
        return have[0] if have.ndim == blocks.ndim else have


def pick(parts, at, axis):
    return lax.dynamic_index_in_dim(parts, at, axis, keepdims=False)


def by_core(core, own, other, axis):
    return jnp.where(
        core == 0, jnp.concatenate([own, other], axis), jnp.concatenate([other, own], axis)
    )


def normalize(rows):
    average = jnp.mean(rows, -1, keepdims=True)
    centered = rows - average
    scale = lax.rsqrt(jnp.mean(centered * centered, -1, keepdims=True) + EPS)
    return centered * scale, scale


def normalize_back(grads, normal, scale):
    return (
        grads
        - jnp.mean(grads, -1, keepdims=True)
        - normal * jnp.mean(grads * normal, -1, keepdims=True)
    ) * scale


def local(mesh):
    def run(
        layer_in, doc_ids, in_proj, out_proj, vec_bias, norm_gain, ffn_in, ffn_bias, ffn_out, out_grad
    ):
        links = Links(mesh)
        core, chips = links.core, links.chips
        side = (links.own // 2) % 2
        slots, shard, _ = layer_in.shape
        assert slots == 2 and mesh.shape["narrow"] == 4
        own_rows = in_proj.shape[1]
        chip_rows = 2 * own_rows
        hidden = ffn_out.shape[0]

        trio_cols = in_proj.reshape(3, own_rows, 2, 3, PAIR).transpose(1, 2, 3, 0, 4)
        trio_cols = trio_cols.reshape(own_rows, 2, 3 * TRIO)
        ffn_cols = ffn_in.reshape(own_rows, chips, 2, hidden).transpose(0, 2, 1, 3)
        ffn_cols = ffn_cols.reshape(own_rows, 2, chips * hidden)
        vectors = jnp.concatenate([vec_bias, norm_gain], 0).T
        vectors = jnp.pad(vectors, ((0, 0), (0, SMALL - 8)))
        cols = jnp.concatenate([trio_cols, ffn_cols], 2)
        mine = jnp.concatenate([pick(cols, core, 1), vectors], 1)
        other = jnp.concatenate([pick(cols, 1 - core, 1), vectors], 1)
        cols = by_core(core, mine, links.core_swap(other), 0)
        split = 3 * TRIO
        out_part = out_proj.reshape(own_rows, 2, HALF).transpose(1, 0, 2).reshape(chip_rows, HALF)
        small = jnp.concatenate(
            [
                cols[:, split + FF // 2 :][:, :8],
                ffn_bias.reshape(chip_rows, 2),
                jnp.zeros((chip_rows, SMALL - 10), BF),
            ],
            1,
        )

        keep = pick(layer_in, side, 0)
        tokens = jnp.concatenate([keep, links.row_swap(pick(layer_in, 1 - side, 0))], 0)
        attn_pack = links.gather(jnp.concatenate([cols[:, :split], out_part, small], 1))
        all_tokens = jnp.concatenate([tokens, links.core_swap(tokens)], 0)
        down_weight = links.gather(ffn_out).reshape(chips * hidden, D)
        up_weight = links.gather(cols[:, split : split + FF // 2]).reshape(D, FF // 2)
        keep = pick(out_grad, side, 0)
        grad_out = jnp.concatenate([keep, links.row_swap(pick(out_grad, 1 - side, 0))], 0)
        grad_out = grad_out.astype(F32)

        trio_weight = attn_pack[..., :split].reshape(D, split)
        out_own = attn_pack[..., split : split + HALF].reshape(chips, 2, own_rows, HALF)
        out_own = out_own.transpose(0, 2, 1, 3).reshape(chips, 1, own_rows, D)
        out_weight = by_core(core, out_own, links.core_swap(out_own), 1).reshape(D, D)
        small = attn_pack[..., split + HALF :]
        bias = small[..., :8].reshape(D, 8).T.astype(F32)
        up_bias = small[..., 8:10].reshape(FF // 2).astype(F32)

        slot_ids = pick(doc_ids, side, 0).reshape(2, 2, shard)
        slot_ids = jnp.stack(
            [
                slot_ids[side, core],
                slot_ids[1 - side, core],
                slot_ids[side, 1 - core],
                slot_ids[1 - side, 1 - core],
            ]
        )
        id_col = slot_ids.reshape(-1, 1)
        id_row = slot_ids.reshape(1, -1)

        own_bias = pick(bias[:2].reshape(2, 2, 3, PAIR), core, 1)
        zero = jnp.zeros_like(own_bias[0])
        trio_bias = jnp.stack([own_bias[0], zero, own_bias[1]], 1).reshape(1, split)
        trio_scale = jnp.concatenate([zero + 0.125, zero + 1.0, zero + 1.0], 1).reshape(1, split)
        trios = ((matmul(all_tokens, trio_weight) + trio_bias) * trio_scale).astype(BF)
        mixed_heads, lse = attend(trios, id_col, id_row)
        count = tokens.shape[0]
        mixed = by_core(core, mixed_heads[:count], links.core_swap(mixed_heads[count:]), 1)

        first_sum = tokens.astype(F32) + matmul(mixed, out_weight) + bias[2]
        first_normal, first_scale = normalize(first_sum)
        normed = first_normal * bias[6] + bias[3]
        normed_low = normed.astype(BF)
        all_normed = jnp.concatenate([normed_low, links.core_swap(normed_low)], 0)
        upper = matmul(all_normed, up_weight) + up_bias
        erf_part = 1.0 + lax.erf(upper * 0.7071067811865476)
        active = (0.5 * upper * erf_part).astype(BF)
        partial = matmul(active, down_weight)
        second_sum = (
            normed
            + partial[:count]
            + links.core_swap(partial[count:].astype(BF)).astype(F32)
            + bias[4]
        )
        second_normal, second_scale = normalize(second_sum)
        result = (second_normal * bias[7] + bias[5]).astype(BF)

        def home(rows):
            got = links.row_swap(rows[shard:])
            kept = rows[:shard]
            return jnp.where(side == 0, jnp.stack([kept, got]), jnp.stack([got, kept]))

        layer_out = home(result)

        grad_second = normalize_back(grad_out * bias[7], second_normal, second_scale)
        grad_down = grad_second.astype(BF)
        all_down = jnp.concatenate([grad_down, links.core_swap(grad_down)], 0)
        grad_down_weight = left_inner(active, all_down).astype(BF)
        grad_active = times_transposed(all_down, down_weight)
        slope = 0.5 * erf_part + upper * jnp.exp(-0.5 * upper * upper) * 0.3989422804014327
        grad_upper = (grad_active * slope).astype(BF)
        grad_up_weight = left_inner(all_normed, grad_upper).astype(BF)
        partial = times_transposed(grad_upper, up_weight)
        grad_normed = (
            grad_second
            + partial[:count]
            + links.core_swap(partial[count:].astype(BF)).astype(F32)
        )
        grad_first = normalize_back(grad_normed * bias[6], first_normal, first_scale)
        grad_attn = grad_first.astype(BF)
        grad_out_weight = left_inner(mixed, grad_attn).reshape(chips, 2, own_rows, D)
        grad_mixed = times_transposed(grad_attn, out_weight).astype(BF).reshape(count, 2, HALF)
        grad_heads = jnp.concatenate(
            [pick(grad_mixed, core, 1), links.core_swap(pick(grad_mixed, 1 - core, 1))], 0
        )
        grad_trios = attend_back(trios, grad_heads, id_col, id_row, lse)
        grad_trio_weight = left_inner(all_tokens, grad_trios).astype(BF)
        partial = times_transposed(grad_trios, trio_weight)
        grad_tokens = (
            grad_first
            + partial[:count]
            + links.core_swap(partial[count:].astype(BF)).astype(F32)
        )
        grad_in = home(grad_tokens.astype(BF))

        down_total = links.scatter_sum(grad_down_weight.reshape(chips, hidden, D))
        up_total = links.scatter_sum(grad_up_weight.reshape(chips, chip_rows, FF // 2))
        sent = links.core_swap(pick(grad_out_weight, 1 - core, 1).astype(BF))
        out_sum = pick(grad_out_weight, core, 1) + sent.astype(F32)
        out_sum = out_sum.astype(BF).reshape(chips, own_rows, 2, HALF).transpose(0, 2, 1, 3)
        out_sum = out_sum.reshape(chips, chip_rows, HALF)
        trio_sums = jnp.sum(grad_trios.astype(F32), 0).reshape(3, 3, PAIR)
        own_half = jnp.stack([trio_sums[:, 0].reshape(HALF), trio_sums[:, 2].reshape(HALF)])
        none = jnp.zeros_like(own_half)
        sums = jnp.concatenate(
            [
                by_core(core, own_half, none, 1),
                jnp.stack(
                    [
                        jnp.sum(grad_attn.astype(F32), 0),
                        jnp.sum(grad_normed, 0),
                        jnp.sum(grad_down.astype(F32), 0),
                        jnp.sum(grad_out, 0),
                        jnp.sum(grad_normed * first_normal, 0),
                        jnp.sum(grad_out * second_normal, 0),
                    ]
                ),
            ],
            0,
        )
        up_bias_sum = jnp.sum(grad_upper.astype(F32), 0).reshape(chips, chip_rows, 2)
        small = jnp.concatenate(
            [
                sums.T.reshape(chips, chip_rows, 8),
                up_bias_sum,
                jnp.zeros((chips, chip_rows, SMALL - 10), F32),
            ],
            2,
        ).astype(BF)
        attn_total = links.scatter_sum(
            jnp.concatenate(
                [grad_trio_weight.reshape(chips, chip_rows, split), out_sum, small], 2
            )
        )

        up_rows = up_total.reshape(2, own_rows, FF // 2)
        attn_rows = attn_total.reshape(2, own_rows, -1)
        packed = jnp.concatenate([attn_rows[..., :split], attn_rows[..., split + HALF :]], 2)
        mine, other = pick(packed, core, 0), pick(packed, 1 - core, 0)
        got = links.core_swap(other.astype(BF)).astype(F32)
        grad_in_proj = by_core(
            core,
            mine[:, :split].reshape(own_rows, 1, 3, 3, PAIR),
            got[:, :split].reshape(own_rows, 1, 3, 3, PAIR),
            1,
        )
        grad_in_proj = grad_in_proj.transpose(3, 0, 1, 2, 4).reshape(3, own_rows, D)
        grad_out_proj = attn_total[:, split : split + HALF].reshape(2, own_rows, HALF)
        grad_out_proj = grad_out_proj.transpose(1, 0, 2).reshape(own_rows, D)
        vectors = (mine[:, split : split + 8] + got[:, split : split + 8]).T
        grad_ffn_bias = attn_total[:, split + HALF + 8 : split + HALF + 10].reshape(hidden)
        got = links.core_swap(pick(up_rows, 1 - core, 0).astype(BF)).astype(F32)
        grad_ffn_in = by_core(
            core,
            pick(up_rows, core, 0).reshape(own_rows, chips, 1, hidden),
            got.reshape(own_rows, chips, 1, hidden),
            2,
        ).reshape(own_rows, FF)
        return (
            layer_out,
            grad_in,
            grad_in_proj,
            grad_out_proj,
            vectors[:6],
            vectors[6:],
            grad_ffn_in,
            grad_ffn_bias,
            down_total,
        )

    return run


def solution(mesh):
    return jax.shard_map(
        local(mesh),
        mesh=mesh,
        in_specs=(
            P("wide", "narrow", None),
            P("wide", None),
            P(None, AXES, None),
            P(AXES, None),
            P(None, AXES),
            P(None, AXES),
            P(AXES, None),
            P(AXES),
            P(AXES, None),
            P("wide", "narrow", None),
        ),
        out_specs=(
            P("wide", "narrow", None),
            P("wide", "narrow", None),
            P(None, AXES, None),
            P(AXES, None),
            P(None, AXES),
            P(None, AXES),
            P(AXES, None),
            P(AXES),
            P(AXES, None),
        ),
        check_vma=False,
    )
```

time: 1190 us -> 349 us (0.29)
  waiting for transfers between devices: 709 us -> 75.3 us
  blocking collectives: 161 us -> 0 us
  matrix products: 178 us -> 45.6 us
  Pallas kernels: 0 us -> 51.4 us
  starting transfers between devices: 0.65 us -> 36.6 us
  other arithmetic: 35.9 us -> 49.5 us
  between operations: 15.2 us -> 2.69 us
    reduce_scatter x5 -> x0, waiting for transfers between devices: 457 us -> none  [the longest x1 142 us: local(): lax.psum_scatter(grad_weight_in, ('wide', 'narrow'), scatter_dimension=0,...]
    all_gather x6 -> x0, waiting for transfers between devices: 132 us -> none  [the longest x1 64.7 us: local(): lax.all_gather(ffn_out, ('wide', 'narrow'), axis=0, tiled=True)]
    unnamed x13 -> x0, waiting for transfers between devices: 120 us -> none
    dot_general x24 -> x4, matrix products: 112 us -> 17.3 us  [matmul(): return jnp.dot(left, right, preferred_element_type=F32)]
    all_gather x2 -> x0, blocking collectives: 83.2 us -> none  [the longest x1 43.8 us: local(): lax.all_gather(vec_bias, ('wide', 'narrow'), axis=1, tiled=True)]
    unnamed x2 -> x0, blocking collectives: 78.1 us -> none
    ppermute x0 -> x41, waiting for transfers between devices: none -> 75.3 us  [send(): return lax.ppermute(value, AXES, pairs)]
    pallas_call x0 -> x2, Pallas kernels: none -> 51.4 us  [the longest x1 29.8 us: attend_back(): pl.pallas_call(attend_back_kernel, grid=(pairs,), in_specs=[pl.BlockSpec(...]
  transfers between devices with their start and end apart: 12 -> 41, of which waited for: 9 -> 12; matrix products, arithmetic and copies ran while one was open for 8% -> 43% of each run, Pallas kernels for 0% -> 15%
where the time goes in v1:
time: 349 us; the launch traced here: 344 us
  local copies, waits for them, and re-layouts  83.5 us (24%)
  waiting for transfers between devices  75.3 us (22%)
  Pallas kernels  51.4 us (15%)
  other arithmetic  49.5 us (14%)
  matrix products  45.6 us (13%)
  starting transfers between devices  36.6 us (10%)
    ppermute x41, waiting for transfers between devices, send(): return lax.ppermute(value, AXES, pairs)  75.3 us
    ppermute x41, starting transfers between devices, send(): return lax.ppermute(value, AXES, pairs)  36.6 us
    pallas_call x1, Pallas kernels, attend_back(): pl.pallas_call(attend_back_kernel, grid=(pairs,), in_specs=[pl.BlockSpec(...  29.8 us
    pallas_call x1, Pallas kernels, attend(): pl.pallas_call(attend_kernel, grid=(pairs,), in_specs=[pl.BlockSpec((tota...  21.6 us
    dynamic_update_slice x24, local copies, waits for them, and re-layouts, put(): return lax.dynamic_update_slice_in_dim(full, piece[:, None], at, 1)  18.5 us
    dot_general x4, matrix products, matmul(): return jnp.dot(left, right, preferred_element_type=F32)  17.3 us
    dot_general x4, matrix products, times_transposed(): lax.dot_general(left, right, (((1,), (1,)), ((), ())), preferred_element_...  15 us
    dot_general x4, matrix products, left_inner(): lax.dot_general(left, right, (((0,), (0,)), ((), ())), preferred_element_...  13.4 us
  transfers between devices with their start and end apart: 41, of which 12 were waited for; matrix products, arithmetic and copies ran while one was open for 43% of the time, Pallas kernels for 15%

profile of v1, /device:TPU:0, one launch (start us, length us, event | category | flops | bytes accessed | tf_op | source)
XLA Modules:
  0.0 344.5 jit_solution(14167123832333268875)
XLA Ops:
  0.7 3.1 collective-permute-start.14
  11.4 1.6 collective-permute-start.3
  14.6 2.2 collective-permute-start.15
  17.7 8.8 %collective-permute-done.10 = bf16[1,48,1536]{2,1,0:T(8,128)(2,1)S(1)} collective-permute-done((bf16[1,48,1536]{2,1,0:T(8,128)(2,1)S(1)}, bf16[1,48,1536]{2,1,0:T(8,128)(2,1)S(1)}, u32[]{:S(2)}, u32[]{:S(2)}) %collective-permute-start.10) | collective-permute-done | bytes 147488 | tf_op jit(solution)/shard_map/ppermute | solution.py:158
  26.8 2.9 collective-permute-start.4
  29.7 1.9 pad_maximum_fusion.13
  32.5 4.8 %collective-permute-done.11 = bf16[2,1,48,1536]{3,2,1,0:T(8,128)(2,1)S(1)} collective-permute-done((bf16[2,1,48,1536]{3,2,1,0:T(8,128)(2,1)S(1)}, bf16[2,1,48,1536]{3,2,1,0:T(8,128)(2,1)S(1)}, u32[]{:S(2)}, u32[]{:S(2)}) %collective-permute-start.11) | collective-permute-done | bytes 294944 | tf_op jit(solution)/shard_map/ppermute | solution.py:158
  38.0 1.6 broadcast_in_dim.67
  40.5 3.5 %collective-permute-done.4 = bf16[2,1,48,1664]{3,2,1,0:T(8,128)(2,1)S(1)} collective-permute-done((bf16[2,1,48,1664]{3,2,1,0:T(8,128)(2,1)S(1)}, bf16[2,1,48,1664]{3,2,1,0:T(8,128)(2,1)S(1)}, u32[]{:S(2)}, u32[]{:S(2)}) %collective-permute-start.4) | collective-permute-done | bytes 319520 | tf_op jit(solution)/shard_map/ppermute | solution.py:158
  47.5 3.2 pad_maximum_fusion.6
  52.2 1.9 bitcast_dynamic-update-slice_fusion
  54.1 6.4 %collective-permute-done.5 = bf16[4,48,1664]{2,1,0:T(8,128)(2,1)} collective-permute-done((bf16[4,48,1664]{2,1,0:T(8,128)(2,1)S(1)}, bf16[4,48,1664]{2,1,0:T(8,128)(2,1)}, u32[]{:S(2)}, u32[]{:S(2)}) %collective-permute-start.5) | collective-permute-done | bytes 639008 | tf_op jit(solution)/shard_map/ppermute | solution.py:158
  60.5 2.4 pad_maximum_fusion.3
  62.9 2.4 collective-permute-start.6
  65.3 2.2 pad_maximum_fusion.5
  67.5 1.9 bitcast_dynamic-update-slice_fusion.2
  69.5 1.8 copy.252
  71.3 1.5 constant_dynamic-update-slice_fusion.6
  72.8 1.9 fusion.29
  74.8 6.2 %collective-permute-done.6 = bf16[2,4,48,1664]{3,2,1,0:T(8,128)(2,1)} collective-permute-done((bf16[2,4,48,1664]{3,2,1,0:T(8,128)(2,1)}, bf16[2,4,48,1664]{3,2,1,0:T(8,128)(2,1)}, u32[]{:S(2)}, u32[]{:S(2)}) %collective-permute-start.6) | collective-permute-done | bytes 1277984 | tf_op jit(solution)/shard_map/ppermute | solution.py:158
  80.9 2.2 slice_bitcast_fusion.2
  84.1 1.8 copy.254
  85.9 1.5 constant_dynamic-update-slice_fusion.5
  87.5 1.5 constant_dynamic-update-slice_fusion.4
  89.0 4.9 %slice.274 = bf16[16,48,1152]{1,2,0:T(8,128)(2,1)} slice(bf16[16,48,1664]{1,2,0:T(8,128)(2,1)} %bitcast.301), slice={[0:16], [0:48], [0:1152]} | slice | bytes 3538944 | tf_op jit(solution)/shard_map/slice | solution.py:281
  96.5 5.7 %copy.255 = bf16[16,48,1152]{2,1,0:T(8,128)(2,1)} copy(bf16[16,48,1152]{1,2,0:T(8,128)(2,1)} %slice.274) | data formatting | bytes 3538944 | tf_op jit(solution)/shard_map/slice | solution.py:281
  104.2 5.5 %multiply_convert_fusion.1.trio_ref = bf16[1024,1152]{1,0:T(8,128)(2,1)} fusion(bf16[768,1152]{1,0:T(8,128)(2,1)} %bitcast.320, f32[1152]{0:T(1024)S(1)} %copy-done.55, f32[1152]{0:T(1024)S(1)} %add.353, bf16[512,768]{1,0:T(8,128)(2,1)} %collective-permute-done.1, bf16[256,768]{1,0:T(8,128)(2,1)} %collective-permute-done, bf16[256,768]{1,0:T(8,128)(2,1)S(1)} %copy-done.20), kind=kOutput, calls=%fused_computation.10 | convolution fusion | flops 1820196864 | bytes 5710848 | tf_op jit(solution)/shard_map/dot_general | solution.py:24
  109.7 21.6 %attend.1 = (bf16[1024,384]{1,0:T(8,128)(2,1)}, f32[3,2,1024]{2,1,0:T(2,128)}) custom-call(bf16[1024,1152]{1,0:T(8,128)(2,1)} %multiply_convert_fusion.1.trio_ref, s32[1024,1]{1,0:T(8,128)} %bitcast.342, s32[1,1024]{1,0:T(1,128)} %bitcast.356), custom_call_target="tpu_custom_call" | custom-call | flops 6442450944 | bytes 4718592 | tf_op jit(solution)/shard_map/attend/pallas_call | solution.py:61
  132.6 2.0 fusion.28
  135.6 2.2 fusion.79
  138.9 2.0 fusion.31
  140.9 1.9 fusion.30
  144.1 7.0 %multiply_convert_fusion = (bf16[1024,1536]{1,0:T(8,128)(2,1)S(1)}, f32[1024,1536]{1,0:T(8,128)}) fusion(f32[1536]{0:T(1024)S(1)} %reshape.495, bf16[768,1536]{1,0:T(8,128)(2,1)} %bitcast.42, bf16[512,768]{1,0:T(8,128)(2,1)} %collective-permute-done.9, bf16[512,768]{1,0:T(8,128)(2,1)S(1)} %fusion.18), kind=kOutput, calls=%fused_computation.7 | convolution fusion | flops 2428502016 | bytes 13375488 | tf_op jit(solution)/shard_map/dot_general | solution.py:24
  151.1 2.6 fusion.81
  157.8 8.9 %collective-permute-done.20 = bf16[256,768]{1,0:T(8,128)(2,1)S(1)} collective-permute-done((bf16[256,768]{1,0:T(8,128)(2,1)S(1)}, bf16[256,768]{1,0:T(8,128)(2,1)S(1)}, u32[]{:S(2)}, u32[]{:S(2)}) %collective-permute-start.20) | collective-permute-done | bytes 393248 | tf_op jit(solution)/shard_map/ppermute | solution.py:158
  168.1 2.0 fusion.73
  174.6 5.0 %convolution_convert_fusion = bf16[1536,768]{1,0:T(8,128)(2,1)S(1)} fusion(bf16[1024,1536]{1,0:T(8,128)(2,1)} %copy-done.56, bf16[512,768]{1,0:T(8,128)(2,1)} %collective-permute-done.21, bf16[512,768]{1,0:T(8,128)(2,1)} %get-tuple-element.90), kind=kOutput, calls=%fused_computation.11 | convolution fusion | flops 2420244480 | bytes 7077888 | tf_op jit(solution)/shard_map/dot_general | solution.py:32
  181.5 1.8 collective-permute-start.37
  183.2 7.6 %fusion.80 = (bf16[1536]{0:T(1024)(128)(2,1)}, bf16[1024,1536]{1,0:T(8,128)(2,1)S(1)}) fusion(f32[1024,1536]{1,0:T(8,128)} %get-tuple-element.139, f32[1536]{0:T(1024)S(1)} %copy-done.47, bf16[1536,768]{1,0:T(8,128)(2,1)S(1)} %bitcast.310, bf16[512,768]{1,0:T(8,128)(2,1)} %collective-permute-done.21, bf16[512,768]{1,0:T(8,128)(2,1)} %get-tuple-element.90), kind=kOutput, calls=%fused_computation.251 | convolution fusion | flops 2437937664 | bytes 13378560 | tf_op jit(solution)/shard_map/dot_general | solution.py:28
  190.9 4.3 %fusion.82 = f32[1024,768]{1,0:T(8,128)S(1)} fusion(bf16[1024,1536]{1,0:T(8,128)(2,1)S(1)} %get-tuple-element.141, bf16[768,1536]{1,0:T(8,128)(2,1)} %bitcast.42), kind=kOutput, calls=%fused_computation.253 | convolution fusion | flops 2415919104 | bytes 8650752 | tf_op jit(solution)/shard_map/dot_general | solution.py:28
  197.1 4.1 %convolution_convert_fusion.1 = bf16[768,1536]{1,0:T(8,128)(2,1)S(1)} fusion(bf16[1024,1536]{1,0:T(8,128)(2,1)S(1)} %get-tuple-element.141, bf16[512,768]{1,0:T(8,128)(2,1)} %collective-permute-done.9, bf16[512,768]{1,0:T(8,128)(2,1)S(1)} %copy-done.30), kind=kOutput, calls=%fused_computation.12 | convolution fusion | flops 2420244480 | bytes 7077888 | tf_op jit(solution)/shard_map/dot_general | solution.py:32
  202.9 1.6 collective-permute-start.32
  204.5 1.8 concatenate.143
  206.3 1.6 copy.278
  207.9 4.6 %multiply_reduce_fusion = (bf16[768]{0:T(1024)(128)(2,1)}, f32[512]{0:T(512)S(1)}, f32[512]{0:T(512)S(1)}, bf16[768]{0:T(1024)(128)(2,1)}, f32[512,768]{1,0:T(8,128)S(1)}, /*index=5*/bf16[512,768]{1,0:T(8,128)(2,1)}) fusion(f32[512,768]{1,0:T(8,128)S(1)} %get-tuple-element.137, f32[512]{0:T(512)S(1)} %add_rsqrt_fusion.1, ...), kind=kLoop, calls=%fused_computation.37 | loop fusion | flops 10221056 | bytes 8679424 | tf_op jit(solution)/shard_map/reduce_sum | solution.py:384
  214.9 1.6 constant_dynamic-slice_fusion.3
  222.1 2.2 fusion.21
  225.2 2.2 fusion.23
  229.5 29.8 %attend_back.1 = bf16[1024,1152]{1,0:T(8,128)(2,1)} custom-call(bf16[1024,1152]{1,0:T(8,128)(2,1)} %multiply_convert_fusion.1.trio_ref, bf16[1024,384]{1,0:T(8,128)(2,1)} %pad_maximum_fusion.15.grad_ref, s32[1024,1]{1,0:T(8,128)} %bitcast.343, s32[1,1024]{1,0:T(1,128)} %bitcast.357, f32[3,2,1024]{2,1,0:T(2,128)} %get-tuple-element.12.lse_ref), custom_call_target="tpu_custom_call" | custom-call | flops 16106127360 | bytes 7077888 | tf_op jit(solution)/shard_map/attend_back/pallas_call | solution.py:121
  259.3 2.2 convert_reduce_fusion
  261.9 3.5 %convolution_convert_fusion.2 = bf16[768,1152]{1,0:T(8,128)(2,1)S(1)} fusion(bf16[1024,1152]{1,0:T(8,128)(2,1)S(1)} %copy-done.12, bf16[512,768]{1,0:T(8,128)(2,1)} %collective-permute-done.1, bf16[256,768]{1,0:T(8,128)(2,1)} %collective-permute-done, bf16[256,768]{1,0:T(8,128)(2,1)S(1)} %copy-done.21), kind=kOutput, calls=%fused_computation.13 | convolution fusion | flops 1817542656 | bytes 5701632 | tf_op jit(solution)/shard_map/dot_general | solution.py:32
  267.6 2.2 fusion.83
  270.8 3.3 maximum_select_fusion.2
  276.4 3.4 concatenate.144
  280.8 1.6 fusion.22
  282.6 1.8 fusion.24
  284.4 2.8 collective-permute-start.34
  290.2 3.0 collective-permute-done.39
  294.1 11.5 %collective-permute-done.34 = bf16[2,1,48,1536]{3,2,1,0:T(8,128)(2,1)S(1)} collective-permute-done((bf16[2,1,48,1536]{3,2,1,0:T(8,128)(2,1)S(1)}, bf16[2,1,48,1536]{3,2,1,0:T(8,128)(2,1)S(1)}, u32[]{:S(2)}, u32[]{:S(2)}) %collective-permute-start.34) | collective-permute-done | bytes 294944 | tf_op jit(solution)/shard_map/ppermute | solution.py:158
  306.6 4.3 %collective-permute-done.35 = bf16[1,48,1536]{2,1,0:T(8,128)(2,1)S(1)} collective-permute-done((bf16[1,48,1536]{2,1,0:T(8,128)(2,1)S(1)}, bf16[1,48,1536]{2,1,0:T(8,128)(2,1)S(1)}, u32[]{:S(2)}, u32[]{:S(2)}) %collective-permute-start.35) | collective-permute-done | bytes 147488 | tf_op jit(solution)/shard_map/ppermute | solution.py:158
  311.0 5.4 %collective-permute-done.28 = bf16[4,48,1664]{2,1,0:T(8,128)(2,1)S(1)} collective-permute-done((bf16[4,48,1664]{2,1,0:T(8,128)(2,1)S(1)}, bf16[4,48,1664]{2,1,0:T(8,128)(2,1)S(1)}, u32[]{:S(2)}, u32[]{:S(2)}) %collective-permute-start.28) | collective-permute-done | bytes 639008 | tf_op jit(solution)/shard_map/ppermute | solution.py:158
  317.8 2.9 collective-permute-start.29
  322.4 10.3 %collective-permute-done.29 = bf16[2,1,48,1664]{3,2,1,0:T(8,128)(2,1)} collective-permute-done((bf16[2,1,48,1664]{3,2,1,0:T(8,128)(2,1)S(1)}, bf16[2,1,48,1664]{3,2,1,0:T(8,128)(2,1)}, u32[]{:S(2)}, u32[]{:S(2)}) %collective-permute-start.29) | collective-permute-done | bytes 319520 | tf_op jit(solution)/shard_map/ppermute | solution.py:158
  336.8 2.2 collective-permute-done.30
  (345 shorter events, 77.5 us)
Async XLA Ops:
  0.6 8.9 %copy-start = (s32[2,1024]{1,0:T(2,128)S(1)}, s32[2,1024]{1,0:T(2,128)}, u32[]{:S(2)}) copy-start(s32[2,1024]{1,0:T(2,128)} %param.11) | copy-start | bytes 24580
  0.7 5.7 %copy-start.50 = (bf16[6,24]{1,0:T(8,128)(2,1)S(1)}, bf16[6,24]{1,0:T(8,128)(2,1)}, u32[]{:S(2)}) copy-start(bf16[6,24]{1,0:T(8,128)(2,1)} %param.14) | copy-start | bytes 868
  0.7 5.7 %copy-start.51 = (bf16[2,24]{1,0:T(2,128)(2,1)S(1)}, bf16[2,24]{1,0:T(2,128)(2,1)}, u32[]{:S(2)}) copy-start(bf16[2,24]{1,0:T(2,128)(2,1)} %param.15) | copy-start | bytes 292
  0.7 13.0 %collective-permute-start.14 = (bf16[1,96,768]{2,1,0:T(8,128)(2,1)}, bf16[1,96,768]{2,1,0:T(8,128)(2,1)}, u32[]{:S(2)}, u32[]{:S(2)}) collective-permute-start(bf16[1,96,768]{2,1,0:T(8,128)(2,1)} %bitcast.339), channel_id=1, source_target_pairs={{0,8},{1,17},{2,10},{3,19},{4,12},{5,21},{6,14},{7,23},{8,0},{9,25... | collective-permute-start | bytes 442376 | tf_op jit(solution)/shard_map/ppermute | solution.py:158
  6.5 4.2 %copy-start.37 = (bf16[24,768]{1,0:T(8,128)(2,1)S(1)}, bf16[24,768]{1,0:T(8,128)(2,1)}, u32[]{:S(2)}) copy-start(bf16[24,768]{1,0:T(8,128)(2,1)} %param.13) | copy-start | bytes 110596
  6.5 4.2 %copy-start.52 = (bf16[96]{0:T(256)(128)(2,1)S(1)}, bf16[96]{0:T(256)(128)(2,1)}, u32[]{:S(2)}) copy-start(bf16[96]{0:T(256)(128)(2,1)} %param.17) | copy-start | bytes 580
  6.6 4.5 %copy-start.31 = (bf16[96,768]{1,0:T(8,128)(2,1)S(1)}, bf16[96,768]{1,0:T(8,128)(2,1)}, u32[]{:S(2)}) copy-start(bf16[96,768]{1,0:T(8,128)(2,1)} %param.18) | copy-start | bytes 442372
  6.6 4.5 %collective-permute-start.2 = (bf16[24,2816]{1,0:T(8,128)(2,1)S(1)}, bf16[24,2816]{1,0:T(8,128)(2,1)S(1)}, u32[]{:S(2)}, u32[]{:S(2)}) collective-permute-start(bf16[24,2816]{1,0:T(8,128)(2,1)S(1)} %pad_maximum_fusion.24), channel_id=1, source_target_pairs={{0,1},{1,0},{2,3},{3,2},{4,5},{5,4},{6,7},{7,6},{8,9},{9,8},{10,11... | collective-permute-start | bytes 405512 | tf_op jit(solution)/shard_map/ppermute | solution.py:158
  8.1 21.6 %copy-start.19 = (bf16[256,768]{1,0:T(8,128)(2,1)}, bf16[256,768]{1,0:T(8,128)(2,1)S(1)}, u32[]{:S(2)}) copy-start(bf16[256,768]{1,0:T(8,128)(2,1)S(1)} %get-tuple-element.122) | copy-start | bytes 1179652
  8.1 21.6 %collective-permute-start = (bf16[256,768]{1,0:T(8,128)(2,1)}, bf16[256,768]{1,0:T(8,128)(2,1)}, u32[]{:S(2)}, u32[]{:S(2)}) collective-permute-start(bf16[256,768]{1,0:T(8,128)(2,1)} %get-tuple-element.123), channel_id=1, source_target_pairs={{0,2},{1,3},{2,0},{3,1},{4,6},{5,7},{6,4},{7,5},{8,10},{9,11},{10,... | collective-permute-start | bytes 1179656 | tf_op jit(solution)/shard_map/ppermute | solution.py:158
  11.4 15.3 %collective-permute-start.3 = (bf16[1,48,1664]{2,1,0:T(8,128)(2,1)S(1)}, bf16[1,48,1664]{2,1,0:T(8,128)(2,1)S(1)}, u32[]{:S(2)}, u32[]{:S(2)}) collective-permute-start(bf16[1,48,1664]{2,1,0:T(8,128)(2,1)S(1)} %bitcast.324), channel_id=1, source_target_pairs={{0,8},{1,17},{2,10},{3,19},{4,12},{5,21},{6,14},{7,23},{8,0},{9,25... | collective-permute-start | bytes 479240 | tf_op jit(solution)/shard_map/ppermute | solution.py:158
  13.2 13.3 %collective-permute-start.10 = (bf16[1,48,1536]{2,1,0:T(8,128)(2,1)S(1)}, bf16[1,48,1536]{2,1,0:T(8,128)(2,1)S(1)}, u32[]{:S(2)}, u32[]{:S(2)}) collective-permute-start(bf16[1,48,1536]{2,1,0:T(8,128)(2,1)S(1)} %get-tuple-element.125), channel_id=1, source_target_pairs={{0,8},{1,17},{2,10},{3,19},{4,12},{5,21},{6,14},{7,23},{8,0},{9,25... | collective-permute-start | bytes 442376 | tf_op jit(solution)/shard_map/ppermute | solution.py:158
  14.6 17.0 %collective-permute-start.15 = (bf16[2,1,96,768]{3,2,1,0:T(8,128)(2,1)S(1)}, bf16[2,1,96,768]{3,2,1,0:T(8,128)(2,1)S(1)}, u32[]{:S(2)}, u32[]{:S(2)}) collective-permute-start(bf16[2,1,96,768]{3,2,1,0:T(8,128)(2,1)S(1)} %pad_maximum_fusion.21), channel_id=1, source_target_pairs={{0,16},{1,9},{2,18},{3,11},{4,20},{5,13},{6,22},{7,15},{8,24},{9,1... | collective-permute-start | bytes 884744 | tf_op jit(solution)/shard_map/ppermute | solution.py:158
  26.5 10.8 %collective-permute-start.11 = (bf16[2,1,48,1536]{3,2,1,0:T(8,128)(2,1)S(1)}, bf16[2,1,48,1536]{3,2,1,0:T(8,128)(2,1)S(1)}, u32[]{:S(2)}, u32[]{:S(2)}) collective-permute-start(bf16[2,1,48,1536]{3,2,1,0:T(8,128)(2,1)S(1)} %pad_maximum_fusion.20), channel_id=1, source_target_pairs={{0,16},{1,9},{2,18},{3,11},{4,20},{5,13},{6,22},{7,15},{8,24},{9,1... | collective-permute-start | bytes 884744 | tf_op jit(solution)/shard_map/ppermute | solution.py:158
  26.8 17.2 %collective-permute-start.4 = (bf16[2,1,48,1664]{3,2,1,0:T(8,128)(2,1)S(1)}, bf16[2,1,48,1664]{3,2,1,0:T(8,128)(2,1)S(1)}, u32[]{:S(2)}, u32[]{:S(2)}) collective-permute-start(bf16[2,1,48,1664]{3,2,1,0:T(8,128)(2,1)S(1)} %pad_maximum_fusion.18), channel_id=1, source_target_pairs={{0,16},{1,9},{2,18},{3,11},{4,20},{5,13},{6,22},{7,15},{8,24},{9,1... | collective-permute-start | bytes 958472 | tf_op jit(solution)/shard_map/ppermute | solution.py:158
  31.6 72.6 %collective-permute-start.1 = (bf16[512,768]{1,0:T(8,128)(2,1)}, bf16[512,768]{1,0:T(8,128)(2,1)}, u32[]{:S(2)}, u32[]{:S(2)}) collective-permute-start(bf16[512,768]{1,0:T(8,128)(2,1)} %pad_maximum_fusion.13), channel_id=1, source_target_pairs={{0,1},{1,0},{2,3},{3,2},{4,5},{5,4},{6,7},{7,6},{8,9},{9,8},{10,11... | collective-permute-start | bytes 2359304 | tf_op jit(solution)/shard_map/ppermute | solution.py:158
  31.7 15.8 %collective-permute-start.16 = (bf16[4,96,768]{2,1,0:T(8,128)(2,1)S(1)}, bf16[4,96,768]{2,1,0:T(8,128)(2,1)}, u32[]{:S(2)}, u32[]{:S(2)}) collective-permute-start(bf16[4,96,768]{2,1,0:T(8,128)(2,1)S(1)} %bitcast.308), channel_id=1, source_target_pairs={{0,2},{1,5},{2,0},{3,7},{4,6},{5,1},{6,4},{7,3},{8,10},{9,13},{10,... | collective-permute-start | bytes 1769480 | tf_op jit(solution)/shard_map/ppermute | solution.py:158
  32.5 12.0 %copy-start.9 = (bf16[4,4,96,768]{3,2,1,0:T(8,128)(2,1)}, bf16[4,4,96,768]{3,2,1,0:T(8,128)(2,1)S(1)}, u32[]{:S(2)}) copy-start(bf16[4,4,96,768]{3,2,1,0:T(8,128)(2,1)S(1)} %bitcast_dynamic-update-slice_fusion.1) | copy-start | bytes 7077892
  37.4 27.9 %collective-permute-start.12 = (bf16[4,48,1536]{2,1,0:T(8,128)(2,1)S(1)}, bf16[4,48,1536]{2,1,0:T(8,128)(2,1)}, u32[]{:S(2)}, u32[]{:S(2)}) collective-permute-start(bf16[4,48,1536]{2,1,0:T(8,128)(2,1)S(1)} %bitcast.307), channel_id=1, source_target_pairs={{0,2},{1,5},{2,0},{3,7},{4,6},{5,1},{6,4},{7,3},{8,10},{9,13},{10,... | collective-permute-start | bytes 1769480 | tf_op jit(solution)/shard_map/ppermute | solution.py:158
  44.0 16.5 %collective-permute-start.5 = (bf16[4,48,1664]{2,1,0:T(8,128)(2,1)S(1)}, bf16[4,48,1664]{2,1,0:T(8,128)(2,1)}, u32[]{:S(2)}, u32[]{:S(2)}) collective-permute-start(bf16[4,48,1664]{2,1,0:T(8,128)(2,1)S(1)} %bitcast.305), channel_id=1, source_target_pairs={{0,2},{1,5},{2,0},{3,7},{4,6},{5,1},{6,4},{7,3},{8,10},{9,13},{10,... | collective-permute-start | bytes 1916936 | tf_op jit(solution)/shard_map/ppermute | solution.py:158
  47.5 22.0 %copy-start.2 = (bf16[4,4,48,1664]{2,3,1,0:T(8,128)(2,1)}, bf16[4,4,48,1664]{2,3,1,0:T(8,128)(2,1)S(1)}, u32[]{:S(2)}) copy-start(bf16[4,4,48,1664]{2,3,1,0:T(8,128)(2,1)S(1)} %constant_dynamic-update-slice_fusion.7) | copy-start | bytes 7667716
  50.7 22.1 %collective-permute-start.17 = (bf16[2,4,96,768]{3,2,1,0:T(8,128)(2,1)}, bf16[2,4,96,768]{3,2,1,0:T(8,128)(2,1)}, u32[]{:S(2)}, u32[]{:S(2)}) collective-permute-start(bf16[2,4,96,768]{3,2,1,0:T(8,128)(2,1)} %pad_maximum_fusion.6), channel_id=1, source_target_pairs={{0,4},{1,3},{2,6},{3,1},{4,0},{5,7},{6,2},{7,5},{8,12},{9,11},{10,... | collective-permute-start | bytes 3538952 | tf_op jit(solution)/shard_map/ppermute | solution.py:158
  62.9 18.1 %collective-permute-start.6 = (bf16[2,4,48,1664]{3,2,1,0:T(8,128)(2,1)}, bf16[2,4,48,1664]{3,2,1,0:T(8,128)(2,1)}, u32[]{:S(2)}, u32[]{:S(2)}) collective-permute-start(bf16[2,4,48,1664]{3,2,1,0:T(8,128)(2,1)} %pad_maximum_fusion.3), channel_id=1, source_target_pairs={{0,4},{1,3},{2,6},{3,1},{4,0},{5,7},{6,2},{7,5},{8,12},{9,11},{10,... | collective-permute-start | bytes 3833864 | tf_op jit(solution)/shard_map/ppermute | solution.py:158
  67.5 71.4 %collective-permute-start.13 = (bf16[2,4,48,1536]{3,2,1,0:T(8,128)(2,1)}, bf16[2,4,48,1536]{3,2,1,0:T(8,128)(2,1)}, u32[]{:S(2)}, u32[]{:S(2)}) collective-permute-start(bf16[2,4,48,1536]{3,2,1,0:T(8,128)(2,1)} %pad_maximum_fusion.5), channel_id=1, source_target_pairs={{0,4},{1,3},{2,6},{3,1},{4,0},{5,7},{6,2},{7,5},{8,12},{9,11},{10,... | collective-permute-start | bytes 3538952 | tf_op jit(solution)/shard_map/ppermute | solution.py:158
  103.7 31.5 %collective-permute-start.8 = (bf16[16,1,24,768]{3,2,0,1:T(8,128)(2,1)S(1)}, bf16[16,1,24,768]{3,2,0,1:T(8,128)(2,1)S(1)}, u32[]{:S(2)}, u32[]{:S(2)}) collective-permute-start(bf16[16,1,24,768]{3,2,0,1:T(8,128)(2,1)S(1)} %reshape.479), channel_id=1, source_target_pairs={{0,1},{1,0},{2,3},{3,2},{4,5},{5,4},{6,7},{7,6},{8,9},{9,8},{10,11... | collective-permute-start | bytes 1769480 | tf_op jit(solution)/shard_map/ppermute | solution.py:158
  132.5 3.1 collective-permute-start.7
  138.5 5.6 %copy-start.29 = (bf16[512,768]{1,0:T(8,128)(2,1)}, bf16[512,768]{1,0:T(8,128)(2,1)S(1)}, u32[]{:S(2)}) copy-start(bf16[512,768]{1,0:T(8,128)(2,1)S(1)} %fusion.18) | copy-start | bytes 2359300
  138.5 5.6 %collective-permute-start.9 = (bf16[512,768]{1,0:T(8,128)(2,1)S(1)}, bf16[512,768]{1,0:T(8,128)(2,1)}, u32[]{:S(2)}, u32[]{:S(2)}) collective-permute-start(bf16[512,768]{1,0:T(8,128)(2,1)S(1)} %fusion.18), channel_id=1, source_target_pairs={{0,1},{1,0},{2,3},{3,2},{4,5},{5,4},{6,7},{7,6},{8,9},{9,8},{10,11... | collective-permute-start | bytes 2359304 | tf_op jit(solution)/shard_map/ppermute | solution.py:158
  144.0 7.0 %copy-start.46 = (f32[1536]{0:T(1024)}, f32[1536]{0:T(1024)S(1)}, u32[]{:S(2)}) copy-start(f32[1536]{0:T(1024)S(1)} %reshape.495) | copy-start | bytes 18436
  144.1 7.0 %copy-start.10 = (bf16[4,4,96,768]{3,2,1,0:T(8,128)(2,1)S(1)}, bf16[4,4,96,768]{3,2,1,0:T(8,128)(2,1)}, u32[]{:S(2)}) copy-start(bf16[4,4,96,768]{3,2,1,0:T(8,128)(2,1)} %fusion.28) | copy-start | bytes 7077892
  153.8 3.0 collective-permute-start.18
  155.5 12.6 %copy-start.5 = (bf16[256,768]{1,0:T(8,128)(2,1)}, bf16[256,768]{1,0:T(8,128)(2,1)S(1)}, u32[]{:S(2)}) copy-start(bf16[256,768]{1,0:T(8,128)(2,1)S(1)} %get-tuple-element.113) | copy-start | bytes 1179652
  155.5 11.2 %collective-permute-start.20 = (bf16[256,768]{1,0:T(8,128)(2,1)S(1)}, bf16[256,768]{1,0:T(8,128)(2,1)S(1)}, u32[]{:S(2)}, u32[]{:S(2)}) collective-permute-start(bf16[256,768]{1,0:T(8,128)(2,1)S(1)} %get-tuple-element.112), channel_id=1, source_target_pairs={{0,2},{1,3},{2,0},{3,1},{4,6},{5,7},{6,4},{7,5},{8,10},{9,11},{10,... | collective-permute-start | bytes 1179656 | tf_op jit(solution)/shard_map/ppermute | solution.py:158
  157.5 10.6 %copy-start.34 = (f32[512]{0:T(512)}, f32[512]{0:T(512)S(1)}, u32[]{:S(2)}) copy-start(f32[512]{0:T(512)S(1)} %broadcast_multiply_fusion.4) | copy-start | bytes 6148
  157.8 12.3 %copy-start.38 = (f32[512]{0:T(512)}, f32[512]{0:T(512)S(1)}, u32[]{:S(2)}) copy-start(f32[512]{0:T(512)S(1)} %add_rsqrt_fusion) | copy-start | bytes 6148
  170.1 4.5 %collective-permute-start.21 = (bf16[512,768]{1,0:T(8,128)(2,1)}, bf16[512,768]{1,0:T(8,128)(2,1)}, u32[]{:S(2)}, u32[]{:S(2)}) collective-permute-start(bf16[512,768]{1,0:T(8,128)(2,1)} %get-tuple-element.90), channel_id=1, source_target_pairs={{0,1},{1,0},{2,3},{3,2},{4,5},{5,4},{6,7},{7,6},{8,9},{9,8},{10,11... | collective-permute-start | bytes 2359304 | tf_op jit(solution)/shard_map/ppermute | solution.py:158
  181.5 40.6 %collective-permute-start.37 = (bf16[2,4,96,768]{3,2,1,0:T(8,128)(2,1)}, bf16[2,4,96,768]{3,2,1,0:T(8,128)(2,1)}, u32[]{:S(2)}, u32[]{:S(2)}) collective-permute-start(bf16[2,4,96,768]{3,2,1,0:T(8,128)(2,1)} %pad_maximum_fusion.8), channel_id=1, source_target_pairs={{0,4},{1,3},{2,6},{3,1},{4,0},{5,7},{6,2},{7,5},{8,12},{9,11},{10,... | collective-permute-start | bytes 3538952 | tf_op jit(solution)/shard_map/ppermute | solution.py:158
  197.1 10.9 %collective-permute-start.22 = (bf16[512,768]{1,0:T(8,128)(2,1)}, bf16[512,768]{1,0:T(8,128)(2,1)}, u32[]{:S(2)}, u32[]{:S(2)}) collective-permute-start(bf16[512,768]{1,0:T(8,128)(2,1)} %slice.421), channel_id=1, source_target_pairs={{0,1},{1,0},{2,3},{3,2},{4,5},{5,4},{6,7},{7,6},{8,9},{9,8},{10,11... | collective-permute-start | bytes 2359304 | tf_op jit(solution)/shard_map/ppermute | solution.py:158
  202.9 22.3 %collective-permute-start.32 = (bf16[2,4,48,1536]{3,2,1,0:T(8,128)(2,1)}, bf16[2,4,48,1536]{3,2,1,0:T(8,128)(2,1)}, u32[]{:S(2)}, u32[]{:S(2)}) collective-permute-start(bf16[2,4,48,1536]{3,2,1,0:T(8,128)(2,1)} %pad_maximum_fusion.7), channel_id=1, source_target_pairs={{0,4},{1,3},{2,6},{3,1},{4,0},{5,7},{6,2},{7,5},{8,12},{9,11},{10,... | collective-permute-start | bytes 3538952 | tf_op jit(solution)/shard_map/ppermute | solution.py:158
  213.1 4.1 %copy-start.3 = (f32[512,768]{1,0:T(8,128)}, f32[512,768]{1,0:T(8,128)S(1)}, u32[]{:S(2)}) copy-start(f32[512,768]{1,0:T(8,128)S(1)} %get-tuple-element.92) | copy-start | bytes 4718596
  216.6 11.9 %collective-permute-start.23 = (bf16[512,384]{1,0:T(8,128)(2,1)S(1)}, bf16[512,384]{1,0:T(8,128)(2,1)S(1)}, u32[]{:S(2)}, u32[]{:S(2)}) collective-permute-start(bf16[512,384]{1,0:T(8,128)(2,1)S(1)} %bitcast.345), channel_id=1, source_target_pairs={{0,1},{1,0},{2,3},{3,2},{4,5},{5,4},{6,7},{7,6},{8,9},{9,8},{10,11... | collective-permute-start | bytes 1179656 | tf_op jit(solution)/shard_map/ppermute | solution.py:158
  218.5 5.8 %copy-start.22 = (f32[768,768]{1,0:T(8,128)}, f32[768,768]{1,0:T(8,128)S(1)}, u32[]{:S(2)}) copy-start(f32[768,768]{1,0:T(8,128)S(1)} %fusion.46) | copy-start | bytes 7077892
  219.4 54.7 %collective-permute-start.26 = (bf16[16,24,768]{2,1,0:T(8,128)(2,1)}, bf16[16,24,768]{2,1,0:T(8,128)(2,1)}, u32[]{:S(2)}, u32[]{:S(2)}) collective-permute-start(bf16[16,24,768]{2,1,0:T(8,128)(2,1)} %fusion.27), channel_id=1, source_target_pairs={{0,1},{1,0},{2,3},{3,2},{4,5},{5,4},{6,7},{7,6},{8,9},{9,8},{10,11... | collective-permute-start | bytes 1769480 | tf_op jit(solution)/shard_map/ppermute | solution.py:158
  221.0 49.8 %collective-permute-start.19 = (bf16[256,768]{1,0:T(8,128)(2,1)}, bf16[256,768]{1,0:T(8,128)(2,1)}, u32[]{:S(2)}, u32[]{:S(2)}) collective-permute-start(bf16[256,768]{1,0:T(8,128)(2,1)} %get-tuple-element.119), channel_id=1, source_target_pairs={{0,2},{1,3},{2,0},{3,1},{4,6},{5,7},{6,4},{7,5},{8,10},{9,11},{10,... | collective-permute-start | bytes 1179656 | tf_op jit(solution)/shard_map/ppermute | solution.py:158
  224.3 56.5 %collective-permute-start.38 = (bf16[4,96,768]{2,1,0:T(8,128)(2,1)}, bf16[4,96,768]{2,1,0:T(8,128)(2,1)}, u32[]{:S(2)}, u32[]{:S(2)}) collective-permute-start(bf16[4,96,768]{2,1,0:T(8,128)(2,1)} %fusion.21), channel_id=1, source_target_pairs={{0,2},{1,5},{2,0},{3,7},{4,6},{5,1},{6,4},{7,3},{8,10},{9,13},{10,... | collective-permute-start | bytes 1769480 | tf_op jit(solution)/shard_map/ppermute | solution.py:158
  227.4 55.1 %collective-permute-start.33 = (bf16[4,48,1536]{2,1,0:T(8,128)(2,1)}, bf16[4,48,1536]{2,1,0:T(8,128)(2,1)}, u32[]{:S(2)}, u32[]{:S(2)}) collective-permute-start(bf16[4,48,1536]{2,1,0:T(8,128)(2,1)} %fusion.23), channel_id=1, source_target_pairs={{0,2},{1,5},{2,0},{3,7},{4,6},{5,1},{6,4},{7,3},{8,10},{9,13},{10,... | collective-permute-start | bytes 1769480 | tf_op jit(solution)/shard_map/ppermute | solution.py:158
  229.5 32.5 %copy-start.21 = (bf16[256,768]{1,0:T(8,128)(2,1)S(1)}, bf16[256,768]{1,0:T(8,128)(2,1)}, u32[]{:S(2)}) copy-start(bf16[256,768]{1,0:T(8,128)(2,1)} %copy-done.19) | copy-start | bytes 1179652
  269.8 4.3 %copy-start.16 = (f32[1024,768]{1,0:T(8,128)}, f32[1024,768]{1,0:T(8,128)S(1)}, u32[]{:S(2)}) copy-start(f32[1024,768]{1,0:T(8,128)S(1)} %fusion.83) | copy-start | bytes 9437188
  269.8 4.3 %copy-start.23 = (f32[768,768]{1,0:T(8,128)S(1)}, f32[768,768]{1,0:T(8,128)}, u32[]{:S(2)}) copy-start(f32[768,768]{1,0:T(8,128)} %copy-done.22) | copy-start | bytes 7077892
  270.8 16.5 %collective-permute-start.24 = (bf16[512,768]{1,0:T(8,128)(2,1)}, bf16[512,768]{1,0:T(8,128)(2,1)}, u32[]{:S(2)}, u32[]{:S(2)}) collective-permute-start(bf16[512,768]{1,0:T(8,128)(2,1)} %slice.420), channel_id=1, source_target_pairs={{0,1},{1,0},{2,3},{3,2},{4,5},{5,4},{6,7},{7,6},{8,9},{9,8},{10,11... | collective-permute-start | bytes 2359304 | tf_op jit(solution)/shard_map/ppermute | solution.py:158
  280.1 25.6 %collective-permute-start.27 = (bf16[2,4,48,1664]{3,2,1,0:T(8,128)(2,1)S(1)}, bf16[2,4,48,1664]{3,2,1,0:T(8,128)(2,1)S(1)}, u32[]{:S(2)}, u32[]{:S(2)}) collective-permute-start(bf16[2,4,48,1664]{3,2,1,0:T(8,128)(2,1)S(1)} %pad_maximum_fusion.4), channel_id=1, source_target_pairs={{0,4},{1,3},{2,6},{3,1},{4,0},{5,7},{6,2},{7,5},{8,12},{9,11},{10,... | collective-permute-start | bytes 3833864 | tf_op jit(solution)/shard_map/ppermute | solution.py:158
  282.4 4.8 %copy-start.17 = (f32[1024,768]{1,0:T(8,128)S(1)}, f32[1024,768]{1,0:T(8,128)}, u32[]{:S(2)}) copy-start(f32[1024,768]{1,0:T(8,128)} %copy-done.16) | copy-start | bytes 9437188
  282.5 4.8 %copy-start.4 = (f32[512,768]{1,0:T(8,128)S(1)}, f32[512,768]{1,0:T(8,128)}, u32[]{:S(2)}) copy-start(f32[512,768]{1,0:T(8,128)} %copy-done.3) | copy-start | bytes 4718596
  282.5 10.7 %collective-permute-start.39 = (bf16[2,1,96,768]{3,2,1,0:T(8,128)(2,1)S(1)}, bf16[2,1,96,768]{3,2,1,0:T(8,128)(2,1)S(1)}, u32[]{:S(2)}, u32[]{:S(2)}) collective-permute-start(bf16[2,1,96,768]{3,2,1,0:T(8,128)(2,1)S(1)} %pad_maximum_fusion.23), channel_id=1, source_target_pairs={{0,16},{1,9},{2,18},{3,11},{4,20},{5,13},{6,22},{7,15},{8,24},{9,1... | collective-permute-start | bytes 884744 | tf_op jit(solution)/shard_map/ppermute | solution.py:158
  284.4 21.2 %collective-permute-start.34 = (bf16[2,1,48,1536]{3,2,1,0:T(8,128)(2,1)S(1)}, bf16[2,1,48,1536]{3,2,1,0:T(8,128)(2,1)S(1)}, u32[]{:S(2)}, u32[]{:S(2)}) collective-permute-start(bf16[2,1,48,1536]{3,2,1,0:T(8,128)(2,1)S(1)} %pad_maximum_fusion.22), channel_id=1, source_target_pairs={{0,16},{1,9},{2,18},{3,11},{4,20},{5,13},{6,22},{7,15},{8,24},{9,1... | collective-permute-start | bytes 884744 | tf_op jit(solution)/shard_map/ppermute | solution.py:158
  289.5 46.3 %collective-permute-start.25 = (bf16[256,768]{1,0:T(8,128)(2,1)}, bf16[256,768]{1,0:T(8,128)(2,1)S(1)}, u32[]{:S(2)}, u32[]{:S(2)}) collective-permute-start(bf16[256,768]{1,0:T(8,128)(2,1)} %get-tuple-element.115), channel_id=1, source_target_pairs={{0,2},{1,3},{2,0},{3,1},{4,6},{5,7},{6,4},{7,5},{8,10},{9,11},{10,... | collective-permute-start | bytes 1179656 | tf_op jit(solution)/shard_map/ppermute | solution.py:158
  293.2 27.5 %collective-permute-start.40 = (bf16[1,96,768]{2,1,0:T(8,128)(2,1)S(1)}, bf16[1,96,768]{2,1,0:T(8,128)(2,1)S(1)}, u32[]{:S(2)}, u32[]{:S(2)}) collective-permute-start(bf16[1,96,768]{2,1,0:T(8,128)(2,1)S(1)} %fusion.35), channel_id=1, source_target_pairs={{0,8},{1,17},{2,10},{3,19},{4,12},{5,21},{6,14},{7,23},{8,0},{9,25... | collective-permute-start | bytes 442376 | tf_op jit(solution)/shard_map/ppermute | solution.py:158
  305.6 5.2 %collective-permute-start.35 = (bf16[1,48,1536]{2,1,0:T(8,128)(2,1)S(1)}, bf16[1,48,1536]{2,1,0:T(8,128)(2,1)S(1)}, u32[]{:S(2)}, u32[]{:S(2)}) collective-permute-start(bf16[1,48,1536]{2,1,0:T(8,128)(2,1)S(1)} %fusion.38), channel_id=1, source_target_pairs={{0,8},{1,17},{2,10},{3,19},{4,12},{5,21},{6,14},{7,23},{8,0},{9,25... | collective-permute-start | bytes 442376 | tf_op jit(solution)/shard_map/ppermute | solution.py:158
  305.9 10.5 %collective-permute-start.28 = (bf16[4,48,1664]{2,1,0:T(8,128)(2,1)S(1)}, bf16[4,48,1664]{2,1,0:T(8,128)(2,1)S(1)}, u32[]{:S(2)}, u32[]{:S(2)}) collective-permute-start(bf16[4,48,1664]{2,1,0:T(8,128)(2,1)S(1)} %fusion.19), channel_id=1, source_target_pairs={{0,2},{1,5},{2,0},{3,7},{4,6},{5,1},{6,4},{7,3},{8,10},{9,13},{10,... | collective-permute-start | bytes 1916936 | tf_op jit(solution)/shard_map/ppermute | solution.py:158
  310.9 11.0 %collective-permute-start.36 = (bf16[24,1536]{1,0:T(8,128)(2,1)S(1)}, bf16[24,1536]{1,0:T(8,128)(2,1)S(1)}, u32[]{:S(2)}, u32[]{:S(2)}) collective-permute-start(bf16[24,1536]{1,0:T(8,128)(2,1)S(1)} %fusion.52), channel_id=1, source_target_pairs={{0,1},{1,0},{2,3},{3,2},{4,5},{5,4},{6,7},{7,6},{8,9},{9,8},{10,11... | collective-permute-start | bytes 221192 | tf_op jit(solution)/shard_map/ppermute | solution.py:158
  317.8 15.0 %copy-start.7 = (f32[4,48,1664]{2,1,0:T(8,128)S(1)}, f32[4,48,1664]{2,1,0:T(8,128)}, u32[]{:S(2)}) copy-start(f32[4,48,1664]{2,1,0:T(8,128)} %copy-done.6) | copy-start | bytes 3833860
  317.8 14.9 %collective-permute-start.29 = (bf16[2,1,48,1664]{3,2,1,0:T(8,128)(2,1)S(1)}, bf16[2,1,48,1664]{3,2,1,0:T(8,128)(2,1)}, u32[]{:S(2)}, u32[]{:S(2)}) collective-permute-start(bf16[2,1,48,1664]{3,2,1,0:T(8,128)(2,1)S(1)} %pad_maximum_fusion.19), channel_id=1, source_target_pairs={{0,16},{1,9},{2,18},{3,11},{4,20},{5,13},{6,22},{7,15},{8,24},{9,1... | collective-permute-start | bytes 958472 | tf_op jit(solution)/shard_map/ppermute | solution.py:158
  333.7 5.3 %collective-permute-start.30 = (bf16[1,48,1664]{2,1,0:T(8,128)(2,1)S(1)}, bf16[1,48,1664]{2,1,0:T(8,128)(2,1)S(1)}, u32[]{:S(2)}, u32[]{:S(2)}) collective-permute-start(bf16[1,48,1664]{2,1,0:T(8,128)(2,1)S(1)} %fusion.32), channel_id=1, source_target_pairs={{0,8},{1,17},{2,10},{3,19},{4,12},{5,21},{6,14},{7,23},{8,0},{9,25... | collective-permute-start | bytes 479240 | tf_op jit(solution)/shard_map/ppermute | solution.py:158
  340.1 1.6 collective-permute-start.31
  (34 other events, 69.9 us)

commit v2 on v1

v2 whole, which is shorter than its diff:
```python
import functools

import jax
import jax.numpy as jnp
from jax import lax
from jax.experimental import pallas as pl
from jax.experimental.pallas import tpu as pltpu
from jax.sharding import PartitionSpec as P

D = 768
FF = 3072
DH = 64
PAIR = 128
HALF = D // 2
QB = 256
AXES = ("wide", "narrow")
EPS = 1e-05
BF = jnp.bfloat16
F32 = jnp.float32
MASKED = -1000000000.0
SMALL = 128
BRIEF = pl.CostEstimate(flops=1000, transcendentals=0, bytes_accessed=1000)


def matmul(left, right):
    return jnp.dot(left, right, preferred_element_type=F32)


def times_transposed(left, right):
    return lax.dot_general(left, right, (((1,), (1,)), ((), ())), preferred_element_type=F32)


def left_inner(left, right):
    return lax.dot_general(left, right, (((0,), (0,)), ((), ())), preferred_element_type=F32)


def overlap(low_ref, high_ref, key_block, query_block):
    return (low_ref[key_block] <= high_ref[query_block]) & (
        low_ref[query_block] <= high_ref[key_block]
    )


def tile_ids(id_col_ref, id_row_ref, keys, queries):
    return id_col_ref[keys, :] == id_row_ref[:, queries]


def one_head(rows, head):
    lane = lax.broadcasted_iota(jnp.int32, rows.shape, 1)
    return jnp.where((lane < DH) if head % 2 == 0 else (lane >= DH), rows, jnp.zeros_like(rows))


def attend_kernel(
    low_ref, high_ref, trio_ref, id_col_ref, id_row_ref, mixed_ref, lse_ref, vt_ref, acc_ref, top_ref, mass_ref
):
    total = trio_ref.shape[0]
    heads = HALF // DH
    blocks = total // QB
    vt_ref[...] = trio_ref[:, 2 * HALF :].T
    acc_ref[...] = jnp.zeros_like(acc_ref)
    mass_ref[...] = jnp.zeros_like(mass_ref)
    top_ref[...] = jnp.full_like(top_ref, -jnp.inf)

    def tile(step, carry):
        query_block, key_block = step // blocks, step % blocks

        @pl.when(overlap(low_ref, high_ref, key_block, query_block))
        def _():
            queries = pl.ds(pl.multiple_of(query_block * QB, QB), QB)
            keys = pl.ds(pl.multiple_of(key_block * QB, QB), QB)
            same = tile_ids(id_col_ref, id_row_ref, keys, queries)
            old_tops = top_ref[:, queries]
            old_mass = mass_ref[:, queries]

            def score(head):
                lanes = slice(head // 2 * PAIR, head // 2 * PAIR + PAIR)
                q = one_head(trio_ref[queries, lanes], head)
                k = trio_ref[keys, HALF + lanes.start : HALF + lanes.stop]
                return jnp.where(same, times_transposed(k, q), MASKED)

            scores = [score(head) for head in range(heads)]
            tops = [jnp.maximum(old_tops[h : h + 1], jnp.max(scores[h], 0, keepdims=True)) for h in range(heads)]
            weights = [jnp.exp(scores[h] - tops[h]) for h in range(heads)]
            shrinks = [jnp.exp(old_tops[h : h + 1] - tops[h]) for h in range(heads)]
            masses = [old_mass[h : h + 1] * shrinks[h] + jnp.sum(weights[h], 0, keepdims=True) for h in range(heads)]
            outs = [matmul(vt_ref[h * DH : (h + 1) * DH, keys], weights[h].astype(BF)) for h in range(heads)]
            for h in range(heads):
                rows = slice(h * DH, (h + 1) * DH)
                acc_ref[rows, queries] = acc_ref[rows, queries] * shrinks[h] + outs[h]
            top_ref[:, queries] = jnp.concatenate(tops + [old_tops[heads:]], 0)
            mass_ref[:, queries] = jnp.concatenate(masses + [old_mass[heads:]], 0)

        return carry

    lax.fori_loop(0, blocks * blocks, tile, 0)
    for head in range(heads):
        rows = slice(head * DH, (head + 1) * DH)
        acc_ref[rows, :] = acc_ref[rows, :] / mass_ref[head : head + 1, :]
    mixed_ref[...] = acc_ref[...].T.astype(BF)
    lse_ref[...] = top_ref[...] + jnp.log(mass_ref[...])


def attend(trios, low, high, id_col, id_row):
    total, width = trios.shape
    return pl.pallas_call(
        attend_kernel,
        grid_spec=pltpu.PrefetchScalarGridSpec(
            num_scalar_prefetch=2,
            grid=(1,),
            in_specs=[
                pl.BlockSpec((total, width), lambda p, *_: (0, 0)),
                pl.BlockSpec((total, 1), lambda p, *_: (0, 0)),
                pl.BlockSpec((1, total), lambda p, *_: (0, 0)),
            ],
            out_specs=[
                pl.BlockSpec((total, HALF), lambda p, *_: (0, 0)),
                pl.BlockSpec((8, total), lambda p, *_: (0, 0)),
            ],
            scratch_shapes=[
                pltpu.VMEM((HALF, total), BF),
                pltpu.VMEM((HALF, total), F32),
                pltpu.VMEM((8, total), F32),
                pltpu.VMEM((8, total), F32),
            ],
        ),
        out_shape=[
            jax.ShapeDtypeStruct((total, HALF), BF),
            jax.ShapeDtypeStruct((8, total), F32),
        ],
        cost_estimate=BRIEF,
        name="attend",
    )(low, high, trios, id_col, id_row)


def attend_back_kernel(
    low_ref,
    high_ref,
    trio_ref,
    grad_ref,
    mixed_ref,
    id_col_ref,
    id_row_ref,
    lse_ref,
    out_ref,
    kt_ref,
    inner_ref,
    dq_ref,
    dk_ref,
    dv_ref,
):
    total = trio_ref.shape[0]
    heads = HALF // DH
    blocks = total // QB
    kt_ref[...] = trio_ref[:, HALF : 2 * HALF].T
    dq_ref[...] = jnp.zeros_like(dq_ref)
    dk_ref[...] = jnp.zeros_like(dk_ref)
    dv_ref[...] = jnp.zeros_like(dv_ref)
    lane = lax.broadcasted_iota(jnp.int32, (8, HALF), 1)
    row = lax.broadcasted_iota(jnp.int32, (8, HALF), 0)
    chosen = jnp.where(lane // DH == row, 1.0, 0.0)
    products = grad_ref[...].astype(F32) * mixed_ref[...].astype(F32)
    inner_ref[...] = lax.dot_general(
        chosen,
        products,
        (((1,), (1,)), ((), ())),
        precision=lax.Precision.HIGHEST,
        preferred_element_type=F32,
    )

    def tile(step, carry):
        query_block, key_block = step // blocks, step % blocks

        @pl.when(overlap(low_ref, high_ref, key_block, query_block))
        def _():
            queries = pl.ds(pl.multiple_of(query_block * QB, QB), QB)
            keys = pl.ds(pl.multiple_of(key_block * QB, QB), QB)
            same = tile_ids(id_col_ref, id_row_ref, keys, queries)
            tops = lse_ref[:, queries]
            inner = inner_ref[:, queries]
            q, k, v, g = [], [], [], []
            for head in range(heads):
                lanes = slice(head // 2 * PAIR, head // 2 * PAIR + PAIR)
                q.append(one_head(trio_ref[queries, lanes], head))
                g.append(one_head(grad_ref[queries, lanes], head))
                k.append(trio_ref[keys, HALF + lanes.start : HALF + lanes.stop])
                v.append(trio_ref[keys, 2 * HALF + lanes.start : 2 * HALF + lanes.stop])
            scores = [times_transposed(k[h], q[h]) for h in range(heads)]
            grad_probs = [times_transposed(v[h], g[h]) for h in range(heads)]
            probs = [jnp.where(same, jnp.exp(scores[h] - tops[h : h + 1]), 0.0) for h in range(heads)]
            grad_scores = [(probs[h] * (grad_probs[h] - inner[h : h + 1])).astype(BF) for h in range(heads)]
            probs = [probs[h].astype(BF) for h in range(heads)]
            dq = [matmul(kt_ref[h * DH : (h + 1) * DH, keys], grad_scores[h]) for h in range(heads)]
            dk = [matmul(grad_scores[h], q[h]) for h in range(heads)]
            dv = [matmul(probs[h], g[h]) for h in range(heads)]
            for h in range(heads):
                dq_ref[h * DH : (h + 1) * DH, queries] += dq[h]
            for pair in range(heads // 2):
                lanes = slice(pair * PAIR, pair * PAIR + PAIR)
                dk_ref[keys, lanes] += dk[2 * pair] + dk[2 * pair + 1]
                dv_ref[keys, lanes] += dv[2 * pair] + dv[2 * pair + 1]

        return carry

    lax.fori_loop(0, blocks * blocks, tile, 0)
    out_ref[:, :HALF] = (dq_ref[...].T.astype(BF).astype(F32) * 0.125).astype(BF)
    out_ref[:, HALF : 2 * HALF] = dk_ref[...].astype(BF)
    out_ref[:, 2 * HALF :] = dv_ref[...].astype(BF)


def attend_back(trios, grads, mixed, low, high, id_col, id_row, lse):
    total, width = trios.shape
    return pl.pallas_call(
        attend_back_kernel,
        grid_spec=pltpu.PrefetchScalarGridSpec(
            num_scalar_prefetch=2,
            grid=(1,),
            in_specs=[
                pl.BlockSpec((total, width), lambda p, *_: (0, 0)),
                pl.BlockSpec((total, HALF), lambda p, *_: (0, 0)),
                pl.BlockSpec((total, HALF), lambda p, *_: (0, 0)),
                pl.BlockSpec((total, 1), lambda p, *_: (0, 0)),
                pl.BlockSpec((1, total), lambda p, *_: (0, 0)),
                pl.BlockSpec((8, total), lambda p, *_: (0, 0)),
            ],
            out_specs=pl.BlockSpec((total, width), lambda p, *_: (0, 0)),
            scratch_shapes=[
                pltpu.VMEM((HALF, total), BF),
                pltpu.VMEM((8, total), F32),
                pltpu.VMEM((HALF, total), F32),
                pltpu.VMEM((total, HALF), F32),
                pltpu.VMEM((total, HALF), F32),
            ],
        ),
        out_shape=jax.ShapeDtypeStruct((total, width), BF),
        cost_estimate=BRIEF,
        name="attend_back",
    )(low, high, trios, grads, mixed, id_col, id_row, lse)


def place_kernel(columns, index_ref, *refs):
    count = (len(refs) - 2 - len(columns)) // 2
    pieces, outs = refs[:count], refs[count : count + len(columns)]
    held = refs[count + len(columns) : -2]
    in_sem, out_sem = refs[-2:]
    arriving = [
        pltpu.make_async_copy(pieces[i], held[i], in_sem.at[i]) for i in range(count)
    ]
    for copy in arriving:
        copy.start()
    leaving = []
    for i in range(count):
        arriving[i].wait()
        for j, (start, stop) in enumerate(columns):
            copy = pltpu.make_async_copy(
                held[i].at[:, :, start:stop], outs[j].at[:, index_ref[i]], out_sem.at[i, j]
            )
            copy.start()
            leaving.append(copy)
    for copy in leaving:
        copy.wait()


def place(pieces, index, columns):
    count = len(pieces)
    outer, rows, _ = pieces[0].shape
    anywhere = pl.BlockSpec(memory_space=pl.ANY)
    return pl.pallas_call(
        functools.partial(place_kernel, columns),
        grid_spec=pltpu.PrefetchScalarGridSpec(
            num_scalar_prefetch=1,
            grid=(1,),
            in_specs=[anywhere] * count,
            out_specs=[anywhere] * len(columns),
            scratch_shapes=[pltpu.VMEM(piece.shape, piece.dtype) for piece in pieces]
            + [pltpu.SemaphoreType.DMA((count,)), pltpu.SemaphoreType.DMA((count, len(columns)))],
        ),
        out_shape=[
            jax.ShapeDtypeStruct((outer, count, rows, stop - start), pieces[0].dtype)
            for start, stop in columns
        ],
        cost_estimate=BRIEF,
        name="place",
    )(index, *pieces)


def take_kernel(columns, count, index_ref, *refs):
    arrays = refs[: len(columns)]
    outs = refs[len(columns) : len(columns) + count]
    held = refs[len(columns) + count : -2]
    in_sem, out_sem = refs[-2:]
    arriving = []
    for i in range(count):
        for j, (start, stop) in enumerate(columns):
            copy = pltpu.make_async_copy(
                arrays[j].at[:, index_ref[i]], held[i].at[:, :, start:stop], in_sem.at[i, j]
            )
            copy.start()
            arriving.append(copy)
    leaving = []
    for i in range(count):
        for copy in arriving[i * len(columns) : (i + 1) * len(columns)]:
            copy.wait()
        copy = pltpu.make_async_copy(held[i], outs[i], out_sem.at[i])
        copy.start()
        leaving.append(copy)
    for copy in leaving:
        copy.wait()


def take(arrays, index):
    outer, count, rows, _ = arrays[0].shape
    columns, start = [], 0
    for array in arrays:
        columns.append((start, start + array.shape[3]))
        start += array.shape[3]
    anywhere = pl.BlockSpec(memory_space=pl.ANY)
    return pl.pallas_call(
        functools.partial(take_kernel, tuple(columns), count),
        grid_spec=pltpu.PrefetchScalarGridSpec(
            num_scalar_prefetch=1,
            grid=(1,),
            in_specs=[anywhere] * len(arrays),
            out_specs=[anywhere] * count,
            scratch_shapes=[pltpu.VMEM((outer, rows, start), BF) for _ in range(count)]
            + [pltpu.SemaphoreType.DMA((count, len(arrays))), pltpu.SemaphoreType.DMA((count,))],
        ),
        out_shape=[jax.ShapeDtypeStruct((outer, rows, start), BF)] * count,
        cost_estimate=BRIEF,
        name="take",
    )(index, *arrays)


class Links:
    def __init__(self, mesh):
        self.devices = mesh.shape["wide"] * mesh.shape["narrow"]
        self.chips = self.devices // 2
        bits = self.chips.bit_length() - 1
        assert self.chips == 1 << bits
        self.groups = [(low, 2) for low in range(bits - 2, -1, -2)]
        if bits % 2:
            self.groups.append((0, 1))
        self.own = lax.axis_index(AXES)
        self.chip = self.own // 2
        self.core = self.own % 2

    def send(self, value, flip_even, flip_odd):
        pairs = [(d, d ^ (flip_odd if d % 2 else flip_even)) for d in range(self.devices)]
        return lax.ppermute(value, AXES, pairs)

    def core_swap(self, value):
        return self.send(value, 1, 1)

    def row_swap(self, value):
        return self.send(value, 2, 2)

    def spots(self, low, size):
        place = (self.chip >> low) % (1 << size)
        if size == 1:
            return jnp.stack([place, place ^ 1]).astype(jnp.int32)
        first, second = 1 + self.core, 2 - self.core
        return jnp.stack([place, place ^ first, place ^ second, place ^ 3]).astype(jnp.int32)

    def gather(self, block, high, columns=None):
        width = block.shape[1]
        have = block[None]
        groups = self.groups if high else self.groups[::-1]
        for stage, (low, size) in enumerate(groups):
            if size == 1:
                (one,) = yield (self.send(have, 2 << low, 2 << low),)
                yield ()
                pieces = [have, one]
            else:
                one = self.send(have, 2 << low, 4 << low)
                two = self.send(have, 4 << low, 2 << low)
                one, two = yield (one, two)
                (three,) = yield (self.send(one, 4 << low, 2 << low),)
                pieces = [have, one, two, three]
            last = stage == len(groups) - 1
            placed = place(pieces, self.spots(low, size), columns if last and columns else ((0, width),))
            if high:
                placed = [out.reshape((-1,) + out.shape[2:]) for out in placed]
            else:
                placed = [out.reshape(1, -1, out.shape[3]) for out in placed]
            placed = yield tuple(placed)
            have = placed[0]

    def scatter(self, arrays, high):
        groups = self.groups if high else self.groups[::-1]
        for low, size in groups:
            if high:
                parts = [a.reshape((1, 1 << size, -1) + a.shape[2:]) for a in arrays]
            else:
                parts = [a.reshape((-1, 1 << size) + a.shape[1:]) for a in arrays]
            pieces = yield tuple(take(parts, self.spots(low, size)))
            if size == 1:
                (got,) = yield (self.send(pieces[1], 2 << low, 2 << low),)
                yield ()
                have = pieces[0].astype(F32) + got.astype(F32)
            else:
                three = self.send(pieces[3], 4 << low, 2 << low)
                two = self.send(pieces[2], 4 << low, 2 << low)
                three, two = yield (three, two)
                one = (pieces[1].astype(F32) + three.astype(F32)).astype(BF)
                (one,) = yield (self.send(one, 2 << low, 4 << low),)
                have = pieces[0].astype(F32) + two.astype(F32) + one.astype(F32)
            arrays = [have.astype(BF)]
        yield (have[0],)


class Flow:
    def __init__(self, steps):
        self.steps = steps
        self.pending = next(steps)
        self.running = True

    def go(self, values):
        try:
            self.pending = self.steps.send(values)
        except StopIteration:
            self.pending = values
            self.running = False


def release(*flows, ties=()):
    held = lax.optimization_barrier((tuple(flow.pending for flow in flows), ties))
    for flow, values in zip(flows, held[0]):
        flow.go(values)
    return held[1]


def finish(flow):
    while flow.running:
        release(flow)
    return flow.pending


def after(value, others):
    return lax.optimization_barrier((value, others))[0]


def pick(parts, at, axis):
    return lax.dynamic_index_in_dim(parts, at, axis, keepdims=False)


def by_core(core, own, other, axis):
    return jnp.where(
        core == 0, jnp.concatenate([own, other], axis), jnp.concatenate([other, own], axis)
    )


def normalize(rows):
    average = jnp.mean(rows, -1, keepdims=True)
    centered = rows - average
    scale = lax.rsqrt(jnp.mean(centered * centered, -1, keepdims=True) + EPS)
    return centered * scale, scale


def normalize_back(grads, normal, scale):
    return (
        grads
        - jnp.mean(grads, -1, keepdims=True)
        - normal * jnp.mean(grads * normal, -1, keepdims=True)
    ) * scale


def local(mesh):
    def run(
        layer_in, doc_ids, in_proj, out_proj, vec_bias, norm_gain, ffn_in, ffn_bias, ffn_out, out_grad
    ):
        links = Links(mesh)
        core, chips = links.core, links.chips
        side = (links.own // 2) % 2
        slots, shard, _ = layer_in.shape
        assert slots == 2 and mesh.shape["narrow"] == 4
        own_rows = in_proj.shape[1]
        chip_rows = 2 * own_rows
        hidden = ffn_out.shape[0]

        def halves(array):
            parts = array.reshape(array.shape[:-1] + (2, -1))
            return pick(parts, core, parts.ndim - 2), pick(parts, 1 - core, parts.ndim - 2)

        keep = pick(layer_in, side, 0)
        got_tokens = links.row_swap(pick(layer_in, 1 - side, 0))

        split = 3 * HALF
        trio_mine, trio_other = halves(in_proj)
        vectors = jnp.pad(jnp.concatenate([vec_bias, norm_gain], 0).T, ((0, 0), (0, SMALL - 8)))
        mine = jnp.concatenate([trio_mine[0], trio_mine[1], trio_mine[2], vectors], 1)
        other = jnp.concatenate([trio_other[0], trio_other[1], trio_other[2], vectors], 1)
        cols = by_core(core, mine, links.core_swap(other), 0)
        small = jnp.concatenate(
            [
                cols[:, split : split + 8],
                ffn_bias.reshape(chip_rows, 2),
                jnp.zeros((chip_rows, SMALL - 10), BF),
            ],
            1,
        )
        attn_block = jnp.concatenate([cols[:, :split], small], 1)
        attn = Flow(links.gather(attn_block, True, ((0, split), (split, split + SMALL))))
        (got_tokens,) = release(attn, ties=(got_tokens,))
        tokens = jnp.concatenate([keep, got_tokens], 0)
        down = Flow(links.gather(ffn_out, False))
        release(attn, down)
        release(attn)

        ffn_cols = ffn_in.reshape(own_rows, chips, 2, hidden).transpose(0, 2, 1, 3)
        ffn_cols = ffn_cols.reshape(own_rows, 2, chips * hidden)
        out_mine, out_other = halves(out_proj)
        mine = jnp.concatenate([pick(ffn_cols, core, 1), out_mine], 1)
        other = jnp.concatenate([pick(ffn_cols, 1 - core, 1), out_other], 1)
        cols = by_core(core, mine, links.core_swap(other), 0)
        up = Flow(links.gather(cols, True, ((0, FF // 2), (FF // 2, FF // 2 + HALF))))
        all_tokens = jnp.concatenate([tokens, links.core_swap(tokens)], 0)
        release(attn, up, down)
        (all_tokens,) = release(attn, up, down, ties=(all_tokens,))
        (all_tokens,) = release(up, ties=(all_tokens,))
        attn_pack = finish(attn)
        trio_weight = attn_pack[0].reshape(D, split)
        small = attn_pack[1]
        bias = small[..., :8].reshape(D, 8).T.astype(F32)
        up_bias = small[..., 8:10].reshape(FF // 2).astype(F32)

        slot_ids = pick(doc_ids, side, 0).reshape(2, 2, shard)
        slot_ids = jnp.stack(
            [
                slot_ids[side, core],
                slot_ids[1 - side, core],
                slot_ids[side, 1 - core],
                slot_ids[1 - side, 1 - core],
            ]
        )
        id_col = slot_ids.reshape(-1, 1)
        id_row = slot_ids.reshape(1, -1)
        low, high = jnp.min(slot_ids, 1), jnp.max(slot_ids, 1)

        own_bias = pick(bias[:2].reshape(2, 2, HALF), core, 1)
        zero = jnp.zeros_like(own_bias[0])
        trio_bias = jnp.concatenate([own_bias[0], zero, own_bias[1]])
        trio_scale = jnp.concatenate([zero + 0.125, zero + 1.0, zero + 1.0])
        trios = ((matmul(all_tokens, trio_weight) + trio_bias) * trio_scale).astype(BF)
        trios, row_grads = release(up, down, ties=(trios, out_grad))
        got_grads = links.row_swap(pick(row_grads, 1 - side, 0))
        mixed_heads, lse = attend(trios, low, high, id_col, id_row)
        up_weight, out_half = finish(up)
        up_weight = up_weight.reshape(D, FF // 2)
        out_half = out_half.reshape(D, HALF)
        out_weight = by_core(core, out_half, links.core_swap(out_half), 1)
        count = tokens.shape[0]
        mixed = by_core(core, mixed_heads[:count], links.core_swap(mixed_heads[count:]), 1)

        first_sum = tokens.astype(F32) + matmul(mixed, out_weight) + bias[2]
        first_normal, first_scale = normalize(first_sum)
        normed = first_normal * bias[6] + bias[3]
        normed_low = normed.astype(BF)
        all_normed = jnp.concatenate([normed_low, links.core_swap(normed_low)], 0)
        all_normed, got_grads = release(down, ties=(all_normed, got_grads))
        grad_out = jnp.concatenate([pick(row_grads, side, 0), got_grads], 0).astype(F32)
        down_weight = finish(down)[0][0]
        upper = matmul(all_normed, up_weight) + up_bias
        erf_part = 1.0 + lax.erf(upper * 0.7071067811865476)
        active = (0.5 * upper * erf_part).astype(BF)
        partial = matmul(active, down_weight)
        second_sum = (
            normed
            + partial[:count]
            + links.core_swap(partial[count:].astype(BF)).astype(F32)
            + bias[4]
        )
        second_normal, second_scale = normalize(second_sum)
        result = (second_normal * bias[7] + bias[5]).astype(BF)

        def home(rows):
            got = links.row_swap(rows[shard:])
            kept = rows[:shard]
            return jnp.where(side == 0, jnp.stack([kept, got]), jnp.stack([got, kept]))

        layer_out = home(result)

        grad_second = normalize_back(grad_out * bias[7], second_normal, second_scale)
        grad_down = grad_second.astype(BF)
        all_down = jnp.concatenate([grad_down, links.core_swap(grad_down)], 0)
        grad_down_weight = left_inner(active, all_down).astype(BF)
        grad_active = times_transposed(all_down, down_weight)
        slope = 0.5 * erf_part + upper * jnp.exp(-0.5 * upper * upper) * 0.3989422804014327
        grad_upper = (grad_active * slope).astype(BF)
        partial = times_transposed(grad_upper, up_weight)
        down_sum = Flow(links.scatter([grad_down_weight.reshape(chips, hidden, D)], True))
        (partial_got,) = release(down_sum, ties=(links.core_swap(partial[count:].astype(BF)),))
        grad_normed = grad_second + partial[:count] + partial_got.astype(F32)
        grad_up_weight = left_inner(all_normed, grad_upper).astype(BF)
        grad_first = normalize_back(grad_normed * bias[6], first_normal, first_scale)
        grad_attn = grad_first.astype(BF)
        grad_out_weight = left_inner(mixed, grad_attn).astype(BF)
        grad_mixed = times_transposed(grad_attn, out_weight).astype(BF)
        mine, other = halves(grad_mixed)
        grad_heads = jnp.concatenate([mine, links.core_swap(other)], 0)
        mine, other = halves(grad_out_weight)
        out_sum = (mine.astype(F32) + links.core_swap(other).astype(F32)).astype(BF)
        up_sum = Flow(
            links.scatter(
                [
                    grad_up_weight.reshape(chips, chip_rows, FF // 2),
                    out_sum.reshape(chips, chip_rows, HALF),
                ],
                False,
            )
        )
        (grad_heads,) = release(up_sum, ties=(grad_heads,))
        grad_trios = attend_back(trios, grad_heads, mixed_heads, low, high, id_col, id_row, lse)
        (grad_trios,) = release(down_sum, up_sum, ties=(grad_trios,))
        grad_trio_weight = left_inner(all_tokens, grad_trios).astype(BF)
        partial = times_transposed(grad_trios, trio_weight)
        grad_tokens = (
            grad_first
            + partial[:count]
            + links.core_swap(partial[count:].astype(BF)).astype(F32)
        )
        grad_in = home(grad_tokens.astype(BF))

        trio_sums = matmul(jnp.ones((8, grad_trios.shape[0]), BF), grad_trios)[0].reshape(3, HALF)
        own_half = jnp.stack([trio_sums[0], trio_sums[2]])
        none = jnp.zeros_like(own_half)
        sums = jnp.concatenate(
            [
                by_core(core, own_half, none, 1),
                jnp.stack(
                    [
                        jnp.sum(grad_attn.astype(F32), 0),
                        jnp.sum(grad_normed, 0),
                        jnp.sum(grad_down.astype(F32), 0),
                        jnp.sum(grad_out, 0),
                        jnp.sum(grad_normed * first_normal, 0),
                        jnp.sum(grad_out * second_normal, 0),
                    ]
                ),
            ],
            0,
        )
        up_bias_sum = jnp.sum(grad_upper.astype(F32), 0).reshape(chips, chip_rows, 2)
        small = jnp.concatenate(
            [
                sums.T.reshape(chips, chip_rows, 8),
                up_bias_sum,
                jnp.zeros((chips, chip_rows, SMALL - 10), F32),
            ],
            2,
        ).astype(BF)
        attn_sum = Flow(
            links.scatter([grad_trio_weight.reshape(chips, chip_rows, split), small], False)
        )
        release(attn_sum)
        release(down_sum, up_sum)
        release(attn_sum, down_sum, up_sum)
        release(attn_sum, down_sum, up_sum)
        release(attn_sum, down_sum, up_sum)
        down_total = finish(down_sum)[0]
        up_total = finish(up_sum)[0]
        attn_total = finish(attn_sum)[0]

        def both(array):
            rows = array.reshape(2, own_rows, -1)
            other = links.core_swap(pick(rows, 1 - core, 0).astype(BF))
            return pick(rows, core, 0), other.astype(F32)

        mine, got = both(up_total)
        grad_ffn_in = by_core(
            core,
            mine[:, : FF // 2].reshape(own_rows, chips, 1, hidden),
            got[:, : FF // 2].reshape(own_rows, chips, 1, hidden),
            2,
        ).reshape(own_rows, FF)
        grad_out_proj = by_core(core, mine[:, FF // 2 :], got[:, FF // 2 :], 1)
        mine, got = both(attn_total)
        grad_in_proj = jnp.stack(
            [
                by_core(core, mine[:, i * HALF : (i + 1) * HALF], got[:, i * HALF : (i + 1) * HALF], 1)
                for i in range(3)
            ]
        )
        vectors = (mine[:, split : split + 8] + got[:, split : split + 8]).T
        grad_ffn_bias = attn_total[:, split + 8 : split + 10].reshape(hidden)
        return (
            layer_out,
            grad_in,
            grad_in_proj,
            grad_out_proj,
            vectors[:6],
            vectors[6:],
            grad_ffn_in,
            grad_ffn_bias,
            down_total,
        )

    return run


def solution(mesh):
    return jax.shard_map(
        local(mesh),
        mesh=mesh,
        in_specs=(
            P("wide", "narrow", None),
            P("wide", None),
            P(None, AXES, None),
            P(AXES, None),
            P(None, AXES),
            P(None, AXES),
            P(AXES, None),
            P(AXES),
            P(AXES, None),
            P("wide", "narrow", None),
        ),
        out_specs=(
            P("wide", "narrow", None),
            P("wide", "narrow", None),
            P(None, AXES, None),
            P(AXES, None),
            P(None, AXES),
            P(None, AXES),
            P(AXES, None),
            P(AXES),
            P(AXES, None),
        ),
        check_vma=False,
    )
```

time: 349 us -> 334 us (0.957)
  local copies, waits for them, and re-layouts: 83.5 us -> 23.4 us
  starting transfers between devices: 36.6 us -> 74.2 us
  Pallas kernels: 51.4 us -> 71.2 us
  other arithmetic: 49.5 us -> 41 us
  waiting for transfers between devices: 75.3 us -> 70.8 us
    ppermute x41 -> x54, starting transfers between devices: 36.6 us -> 74.2 us  [send(): return lax.ppermute(value, AXES, pairs)]
    pallas_call x2 -> x14, Pallas kernels: 51.4 us -> 71.2 us  [the longest x1 21.7 us: attend_back(): pl.pallas_call(attend_back_kernel, grid_spec=pltpu.PrefetchScalarGridSpec...]
    dynamic_update_slice x24 -> x0, local copies, waits for them, and re-layouts: 18.5 us -> none  [put(): return lax.dynamic_update_slice_in_dim(full, piece[:, None], at, 1)]
    slice x13 -> x9, local copies, waits for them, and re-layouts: 13 us -> 0.38 us  [the longest x1 0.24 us: run(): trio_mine[0]]
    another operation x15 -> x5, other arithmetic: 11.6 us -> 1.99 us  [the longest x2 1.26 us: spots(): jnp.stack([place, place ^ first, place ^ second, place ^ 3])]
    another operation x15 -> x0, local copies, waits for them, and re-layouts: 6.87 us -> none  [the longest x5 6.36 us: put(): return lax.dynamic_update_slice_in_dim(full, piece[:, None], at, 1)]
    broadcast_in_dim x7 -> x1, local copies, waits for them, and re-layouts: 5.11 us -> 0.01 us  [run(): zero = jnp.zeros_like(own_bias[0])]
    concatenate x6 -> x4, local copies, waits for them, and re-layouts: 5.03 us -> 0.2 us  [the longest x1 0.09 us: run(): attn_block = jnp.concatenate([cols[:, :split], small], 1)]
  transfers between devices with their start and end apart: 41 -> 54, of which waited for: 12 -> 26; matrix products, arithmetic and copies ran while one was open for 43% -> 20% of each run, Pallas kernels for 15% -> 19%
where the time goes in v2:
time: 334 us; the launch traced here: 327 us
  starting transfers between devices  74.2 us (22%)
  Pallas kernels  71.2 us (21%)
  waiting for transfers between devices  70.8 us (21%)
  matrix products  44.3 us (13%)
  other arithmetic  41 us (12%)
  local copies, waits for them, and re-layouts  23.4 us (7%)
    ppermute x54, starting transfers between devices, send(): return lax.ppermute(value, AXES, pairs)  74.2 us
    ppermute x54, waiting for transfers between devices, send(): return lax.ppermute(value, AXES, pairs)  70.8 us
    pallas_call x1, Pallas kernels, attend_back(): pl.pallas_call(attend_back_kernel, grid_spec=pltpu.PrefetchScalarGridSpec...  21.7 us
    pallas_call x6, Pallas kernels, take(): pl.pallas_call(functools.partial(take_kernel, tuple(columns), count), gri...  17.8 us
    pallas_call x6, Pallas kernels, place(): pl.pallas_call(functools.partial(place_kernel, columns), grid_spec=pltpu....  17.3 us
    dot_general x4, matrix products, times_transposed(): lax.dot_general(left, right, (((1,), (1,)), ((), ())), preferred_element_...  15.3 us
    dot_general x5, matrix products, matmul(): return jnp.dot(left, right, preferred_element_type=F32)  14.8 us
    pallas_call x1, Pallas kernels, attend(): pl.pallas_call(attend_kernel, grid_spec=pltpu.PrefetchScalarGridSpec(num_...  14.3 us
  transfers between devices with their start and end apart: 54, of which 26 were waited for; matrix products, arithmetic and copies ran while one was open for 20% of the time, Pallas kernels for 19%

profile of v2, /device:TPU:0, one launch (start us, length us, event | category | flops | bytes accessed | tf_op | source)
XLA Modules:
  0.0 327.4 jit_solution(1678670805064277964)
XLA Ops:
  0.7 3.1 collective-permute-start.6
  9.1 1.6 collective-permute-start.1
  10.7 2.6 collective-permute-start.2
  14.0 3.6 %collective-permute-done.1.refs_1_ = bf16[1,48,1280]{2,1,0:T(8,128)(2,1)S(1)} collective-permute-done((bf16[1,48,1280]{2,1,0:T(8,128)(2,1)S(1)}, bf16[1,48,1280]{2,1,0:T(8,128)(2,1)S(1)}, u32[]{:S(2)}, u32[]{:S(2)}) %collective-permute-start.1) | collective-permute-done | bytes 122912 | tf_op jit(solution)/shard_map/ppermute | solution.py:347
  19.0 2.6 collective-permute-start.5
  21.8 4.3 %collective-permute-done.5.refs_3_ = bf16[1,48,1280]{2,1,0:T(8,128)(2,1)S(1)} collective-permute-done((bf16[1,48,1280]{2,1,0:T(8,128)(2,1)S(1)}, bf16[1,48,1280]{2,1,0:T(8,128)(2,1)S(1)}, u32[]{:S(2)}, u32[]{:S(2)}) %collective-permute-start.5) | collective-permute-done | bytes 122912 | tf_op jit(solution)/shard_map/ppermute | solution.py:347
  26.8 2.5 place.6
  31.2 3.4 %collective-permute-start.11 = (bf16[1,48,1920]{2,1,0:T(8,128)(2,1)S(1)}, bf16[1,48,1920]{2,1,0:T(8,128)(2,1)S(1)}, u32[]{:S(2)}, u32[]{:S(2)}) collective-permute-start(bf16[1,48,1920]{2,1,0:T(8,128)(2,1)S(1)} %maximum_select_fusion.7.refs_0_), channel_id=1, source_target_pairs={{0,16},{1,9},{2,18},{3,11},{4,20},{5,13},{6,22},{7,15},{8,24},{9,1... | collective-permute-start | bytes 552968 | tf_op jit(solution)/shard_map/ppermute | solution.py:347
  37.6 2.4 collective-permute-done.11.refs_2_
  42.8 2.9 collective-permute-start.14
  46.4 2.5 place.7
  50.5 2.6 place.8
  57.5 4.1 %collective-permute-start.19 = (bf16[1,384,768]{2,1,0:T(8,128)(2,1)S(1)}, bf16[1,384,768]{2,1,0:T(8,128)(2,1)}, u32[]{:S(2)}, u32[]{:S(2)}) collective-permute-start(bf16[1,384,768]{2,1,0:T(8,128)(2,1)S(1)} %bitcast.177), channel_id=1, source_target_pairs={{0,16},{1,9},{2,18},{3,11},{4,20},{5,13},{6,22},{7,15},{8,24},{9,1... | collective-permute-start | bytes 1769480 | tf_op jit(solution)/shard_map/ppermute | solution.py:347
  61.6 3.0 place.9
  66.1 5.2 %multiply_convert_fusion.1.trio_ref = bf16[1024,1152]{1,0:T(8,128)(2,1)} fusion(bf16[1024,768]{1,0:T(8,128)(2,1)S(1)} %pad_maximum_fusion, bf16[768,1152]{1,0:T(8,128)(2,1)} %bitcast.228, f32[1152]{0:T(1024)S(1)} %copy-done.71, f32[1152]{0:T(1024)S(1)} %pad_maximum_fusion.19), kind=kOutput, calls=%fused_computation.9 | convolution fusion | flops 1815478272 | bytes 5710848 | tf_op jit(solution)/shard_map/dot_general | solution.py:26
  71.3 10.7 %collective-permute-done.18.refs_1_ = bf16[1,384,768]{2,1,0:T(8,128)(2,1)} collective-permute-done((bf16[1,384,768]{2,1,0:T(8,128)(2,1)S(1)}, bf16[1,384,768]{2,1,0:T(8,128)(2,1)}, u32[]{:S(2)}, u32[]{:S(2)}) %collective-permute-start.18) | collective-permute-done | bytes 589856 | tf_op jit(solution)/shard_map/ppermute | solution.py:347
  84.3 14.3 %attend.1 = (bf16[1024,384]{1,0:T(8,128)(2,1)}, f32[8,1024]{1,0:T(8,128)}) custom-call(s32[4]{0:T(128)} %get-tuple-element.270.low_ref, s32[4]{0:T(128)} %get-tuple-element.269.high_ref, bf16[1024,1152]{1,0:T(8,128)(2,1)} %multiply_convert_fusion.1.trio_ref, s32[1024,1]{1,0:T(8,128)} %bitcast.170, s32[1,1024]{1,0:T(1,128)} %bitcast.222), custom_call_target="tpu_custom_call" | custom-call | flops 1000 | bytes 1000 | tf_op jit(solution)/shard_map/attend/pallas_call | solution.py:104
  99.5 3.5 %place.10 = (bf16[4,4,48,1536]{3,2,1,0:T(8,128)(2,1)}, bf16[4,4,48,384]{3,2,1,0:T(8,128)(2,1)}) custom-call(s32[4]{0:T(128)} %pad_add_fusion.2.index_ref, bf16[4,48,1920]{2,1,0:T(8,128)(2,1)} %bitcast.174, bf16[4,48,1920]{2,1,0:T(8,128)(2,1)} %collective-permute-done.16.refs_1_, bf16[4,48,1920]{2,1,0:T(8,128)(2,1)} %collective-permute-done.17.refs_2_, ...), custom_call_target="tpu_custom_call" | custom-call | flops 1000 | bytes 1000 | tf_op jit(solution)/shard_map/place/pallas_call | solution.py:266
  107.8 2.1 collective-permute-start.23
  113.9 2.4 pad_maximum_fusion.1
  116.2 5.0 %collective-permute-done.25 = bf16[256,768]{1,0:T(8,128)(2,1)S(1)} collective-permute-done((bf16[256,768]{1,0:T(8,128)(2,1)}, bf16[256,768]{1,0:T(8,128)(2,1)S(1)}, u32[]{:S(2)}, u32[]{:S(2)}) %collective-permute-start.25) | collective-permute-done | bytes 393248 | tf_op jit(solution)/shard_map/ppermute | solution.py:347
  121.2 2.0 collective-permute-done.23.refs_3_
  123.2 3.2 place.11
  126.4 5.6 %multiply_convert_fusion = (bf16[1024,1536]{1,0:T(8,128)(2,1)S(1)}, f32[1024,1536]{1,0:T(8,128)S(1)}) fusion(f32[1536]{0:T(1024)} %reshape.448, bf16[1024,768]{1,0:T(8,128)(2,1)S(1)} %copy-done.15, bf16[768,1536]{1,0:T(8,128)(2,1)} %bitcast.226), kind=kOutput, calls=%fused_computation.7 | convolution fusion | flops 2425356288 | bytes 13375488 | tf_op jit(solution)/shard_map/dot_general | solution.py:26
  132.0 2.6 fusion.7
  135.1 2.0 collective-permute-done.26
  141.6 2.0 collective-permute-done.28
  143.6 5.8 %fusion.58 = (bf16[1536]{0:T(1024)(128)(2,1)}, bf16[1024,1536]{1,0:T(8,128)(2,1)S(1)}) fusion(f32[1024,1536]{1,0:T(8,128)S(1)} %get-tuple-element.320, f32[1536]{0:T(1024)S(1)} %copy-done.57, bf16[1,1536,768]{2,1,0:T(8,128)(2,1)S(1)} %bitcast.180, bf16[512,768]{1,0:T(8,128)(2,1)S(1)} %collective-permute-done.28, bf16[512,768]{1,0:T(8,128)(2,1)S(1)} %get-tuple-element.272), kind=kOutput, calls=%fused_computation.198 | convolution fusion | flops 2437937664 | bytes 13378560 | tf_op jit(solution)/shard_map/dot_general | solution.py:30
  149.4 2.6 fusion.59
  152.1 1.7 copy-done.12
  155.0 4.2 %convolution_convert_fusion.1 = bf16[1536,768]{1,0:T(8,128)(2,1)} fusion(bf16[1024,1536]{1,0:T(8,128)(2,1)S(1)} %get-tuple-element.319, bf16[512,768]{1,0:T(8,128)(2,1)S(1)} %collective-permute-done.28, bf16[512,768]{1,0:T(8,128)(2,1)S(1)} %get-tuple-element.272), kind=kOutput, calls=%fused_computation.11 | convolution fusion | flops 2420244480 | bytes 7077888 | tf_op jit(solution)/shard_map/dot_general | solution.py:34
  159.1 3.2 take.6
  162.3 4.7 %multiply_reduce_fusion = (bf16[768]{0:T(1024)(128)(2,1)}, f32[512]{0:T(512)S(1)}, f32[512]{0:T(512)S(1)}, bf16[768]{0:T(1024)(128)(2,1)}, f32[512,768]{1,0:T(8,128)S(1)}, /*index=5*/bf16[512,768]{1,0:T(8,128)(2,1)}) fusion(f32[512,768]{1,0:T(8,128)S(1)} %get-tuple-element.318, f32[512]{0:T(512)S(1)} %add_rsqrt_fusion.1, ...), kind=kLoop, calls=%fused_computation.39 | loop fusion | flops 10221056 | bytes 8679424 | tf_op jit(solution)/shard_map/reduce_sum | solution.py:633
  171.2 2.1 convolution_convert_fusion.4
  173.5 1.6 constant_dynamic-slice_fusion.6
  175.6 5.8 %convolution_convert_fusion = bf16[768,1536]{1,0:T(8,128)(2,1)} fusion(bf16[1024,768]{1,0:T(8,128)(2,1)S(1)} %copy-done.16, bf16[1024,1536]{1,0:T(8,128)(2,1)} %copy-done.72), kind=kOutput, calls=%fused_computation.10 | convolution fusion | flops 2417098752 | bytes 7077888 | tf_op jit(solution)/shard_map/dot_general | solution.py:34
  185.6 2.1 fusion.22
  187.7 3.6 %take.7 = (bf16[4,48,1920]{2,1,0:T(8,128)(2,1)}, bf16[4,48,1920]{2,1,0:T(8,128)(2,1)}, bf16[4,48,1920]{2,1,0:T(8,128)(2,1)}, bf16[4,48,1920]{2,1,0:T(8,128)(2,1)}) custom-call(s32[4]{0:T(128)} %pad_add_fusion.2.index_ref, bf16[4,4,48,1536]{3,2,1,0:T(8,128)(2,1)} %bitcast.181, bf16[4,4,48,384]{3,2,1,0:T(8,128)(2,1)} %bitcast.182), custom_call_target="tpu_custom_call" | custom-call | flops 1000 | bytes 1000 | tf_op jit(solution)/shard_map/take/pallas_call | solution.py:316
  191.4 2.0 collective-permute-start.35
  193.5 2.5 collective-permute-start.27
  196.7 9.3 %collective-permute-done.27 = bf16[256,768]{1,0:T(8,128)(2,1)S(1)} collective-permute-done((bf16[256,768]{1,0:T(8,128)(2,1)S(1)}, bf16[256,768]{1,0:T(8,128)(2,1)S(1)}, u32[]{:S(2)}, u32[]{:S(2)}) %collective-permute-start.27) | collective-permute-done | bytes 393248 | tf_op jit(solution)/shard_map/ppermute | solution.py:347
  207.0 21.7 %attend_back.1 = bf16[1024,1152]{1,0:T(8,128)(2,1)} custom-call(s32[4]{0:T(128)} %get-tuple-element.270.low_ref, s32[4]{0:T(128)} %get-tuple-element.269.high_ref, bf16[1024,1152]{1,0:T(8,128)(2,1)} %multiply_convert_fusion.1.trio_ref, bf16[1024,384]{1,0:T(8,128)(2,1)} %pad_maximum_fusion.7.grad_ref, bf16[1024,384]{1,0:T(8,128)(2,1)} %get-tuple-element.131.mixed_ref, ...), custom_call_target="tpu_custom_call" | custom-call | flops 1000 | bytes 1000 | tf_op jit(solution)/shard_map/attend_back/pallas_call | solution.py:211
  228.8 4.7 %fusion.60 = f32[1024,768]{1,0:T(8,128)S(1)} fusion(bf16[1024,1152]{1,0:T(8,128)(2,1)} %attend_back.1, bf16[768,1152]{1,0:T(8,128)(2,1)} %bitcast.229), kind=kOutput, calls=%fused_computation.200 | convolution fusion | flops 1811939328 | bytes 7274496 | tf_op jit(solution)/shard_map/dot_general | solution.py:30
  235.4 11.9 %collective-permute-start.36 = (bf16[512,768]{1,0:T(8,128)(2,1)}, bf16[512,768]{1,0:T(8,128)(2,1)S(1)}, u32[]{:S(2)}, u32[]{:S(2)}) collective-permute-start(bf16[512,768]{1,0:T(8,128)(2,1)} %slice.279), channel_id=1, source_target_pairs={{0,1},{1,0},{2,3},{3,2},{4,5},{5,4},{6,7},{7,6},{8,9},{9,8},{10,11... | collective-permute-start | bytes 2359304 | tf_op jit(solution)/shard_map/ppermute | solution.py:347
  248.9 2.3 add_convert_fusion.4
  251.2 2.4 add_convert_fusion.2
  253.6 1.7 collective-permute-start.41
  256.1 3.5 %convolution_convert_fusion.2 = bf16[768,1152]{1,0:T(8,128)(2,1)} fusion(bf16[1024,768]{1,0:T(8,128)(2,1)S(1)} %copy-done.14, bf16[1024,1152]{1,0:T(8,128)(2,1)S(1)} %copy-done.2), kind=kOutput, calls=%fused_computation.12 | convolution fusion | flops 1812824064 | bytes 5701632 | tf_op jit(solution)/shard_map/dot_general | solution.py:34
  259.6 3.2 take.8
  262.8 3.2 collective-permute-start.38
  266.1 1.6 collective-permute-done.40
  267.7 2.4 fusion.23.refs_0_
  270.1 2.3 add_convert_fusion.3
  272.4 2.6 take.9
  275.0 2.7 take.10
  280.2 2.6 collective-permute-start.43
  282.8 2.9 collective-permute-start.45
  285.8 1.8 fusion.17
  291.4 7.8 %collective-permute-done.46 = bf16[1,48,1920]{2,1,0:T(8,128)(2,1)S(1)} collective-permute-done((bf16[1,48,1920]{2,1,0:T(8,128)(2,1)}, bf16[1,48,1920]{2,1,0:T(8,128)(2,1)S(1)}, u32[]{:S(2)}, u32[]{:S(2)}) %collective-permute-start.46) | collective-permute-done | bytes 184352 | tf_op jit(solution)/shard_map/ppermute | solution.py:347
  299.9 2.1 fusion.24.refs_0_
  303.1 2.5 take.11
  306.0 2.9 collective-permute-start.49
  310.6 2.7 collective-permute-done.49
  313.3 5.1 %collective-permute-done.50 = bf16[1,48,1280]{2,1,0:T(8,128)(2,1)S(1)} collective-permute-done((bf16[1,48,1280]{2,1,0:T(8,128)(2,1)}, bf16[1,48,1280]{2,1,0:T(8,128)(2,1)S(1)}, u32[]{:S(2)}, u32[]{:S(2)}) %collective-permute-start.50) | collective-permute-done | bytes 122912 | tf_op jit(solution)/shard_map/ppermute | solution.py:347
  (357 shorter events, 75.4 us)
Async XLA Ops:
  0.6 81.8 %copy-start = (s32[2,1024]{1,0:T(2,128)S(1)}, s32[2,1024]{1,0:T(2,128)}, u32[]{:S(2)}) copy-start(s32[2,1024]{1,0:T(2,128)} %param.11) | copy-start | bytes 24580
  0.7 21.1 %collective-permute-start.6 = (bf16[1,96,768]{2,1,0:T(8,128)(2,1)}, bf16[1,96,768]{2,1,0:T(8,128)(2,1)S(1)}, u32[]{:S(2)}, u32[]{:S(2)}) collective-permute-start(bf16[1,96,768]{2,1,0:T(8,128)(2,1)} %bitcast.206), channel_id=1, source_target_pairs={{0,2},{1,5},{2,0},{3,7},{4,6},{5,1},{6,4},{7,3},{8,10},{9,13},{10,... | collective-permute-start | bytes 442376 | tf_op jit(solution)/shard_map/ppermute | solution.py:347
  3.8 18.0 %collective-permute-start.7 = (bf16[1,96,768]{2,1,0:T(8,128)(2,1)}, bf16[1,96,768]{2,1,0:T(8,128)(2,1)S(1)}, u32[]{:S(2)}, u32[]{:S(2)}) collective-permute-start(bf16[1,96,768]{2,1,0:T(8,128)(2,1)} %bitcast.207), channel_id=1, source_target_pairs={{0,4},{1,3},{2,6},{3,1},{4,0},{5,7},{6,2},{7,5},{8,12},{9,11},{10,... | collective-permute-start | bytes 442376 | tf_op jit(solution)/shard_map/ppermute | solution.py:347
  7.3 1.6 collective-permute-start
  7.5 11.5 %collective-permute-start.3 = (bf16[256,768]{1,0:T(8,128)(2,1)S(1)}, bf16[256,768]{1,0:T(8,128)(2,1)S(1)}, u32[]{:S(2)}, u32[]{:S(2)}) collective-permute-start(bf16[256,768]{1,0:T(8,128)(2,1)S(1)} %get-tuple-element.293), channel_id=1, source_target_pairs={{0,2},{1,3},{2,0},{3,1},{4,6},{5,7},{6,4},{7,5},{8,10},{9,11},{10,... | collective-permute-start | bytes 1179656 | tf_op jit(solution)/shard_map/ppermute | solution.py:347
  9.1 17.1 %copy-start.28 = (bf16[48,1280]{1,0:T(8,128)(2,1)}, bf16[48,1280]{1,0:T(8,128)(2,1)S(1)}, u32[]{:S(2)}) copy-start(bf16[48,1280]{1,0:T(8,128)(2,1)S(1)} %concatenate.191) | copy-start | bytes 368644
  9.1 8.5 %collective-permute-start.1 = (bf16[1,48,1280]{2,1,0:T(8,128)(2,1)S(1)}, bf16[1,48,1280]{2,1,0:T(8,128)(2,1)S(1)}, u32[]{:S(2)}, u32[]{:S(2)}) collective-permute-start(bf16[1,48,1280]{2,1,0:T(8,128)(2,1)S(1)} %bitcast.200), channel_id=1, source_target_pairs={{0,8},{1,17},{2,10},{3,19},{4,12},{5,21},{6,14},{7,23},{8,0},{9,25... | collective-permute-start | bytes 368648 | tf_op jit(solution)/shard_map/ppermute | solution.py:347
  10.7 6.8 %collective-permute-start.2 = (bf16[1,48,1280]{2,1,0:T(8,128)(2,1)S(1)}, bf16[1,48,1280]{2,1,0:T(8,128)(2,1)S(1)}, u32[]{:S(2)}, u32[]{:S(2)}) collective-permute-start(bf16[1,48,1280]{2,1,0:T(8,128)(2,1)S(1)} %bitcast.201), channel_id=1, source_target_pairs={{0,16},{1,9},{2,18},{3,11},{4,20},{5,13},{6,22},{7,15},{8,24},{9,1... | collective-permute-start | bytes 368648 | tf_op jit(solution)/shard_map/ppermute | solution.py:347
  17.5 12.4 %collective-permute-start.4 = (bf16[24,1920]{1,0:T(8,128)(2,1)S(1)}, bf16[24,1920]{1,0:T(8,128)(2,1)S(1)}, u32[]{:S(2)}, u32[]{:S(2)}) collective-permute-start(bf16[24,1920]{1,0:T(8,128)(2,1)S(1)} %pad_maximum_fusion.17), channel_id=1, source_target_pairs={{0,1},{1,0},{2,3},{3,2},{4,5},{5,4},{6,7},{7,6},{8,9},{9,8},{10,11... | collective-permute-start | bytes 276488 | tf_op jit(solution)/shard_map/ppermute | solution.py:347
  19.0 7.1 %collective-permute-start.5 = (bf16[1,48,1280]{2,1,0:T(8,128)(2,1)S(1)}, bf16[1,48,1280]{2,1,0:T(8,128)(2,1)S(1)}, u32[]{:S(2)}, u32[]{:S(2)}) collective-permute-start(bf16[1,48,1280]{2,1,0:T(8,128)(2,1)S(1)} %collective-permute-done.1.refs_1_), channel_id=1, source_target_pairs={{0,16},{1,9},{2,18},{3,11},{4,20},{5,13},{6,22},{7,15},{8,24},{9,1... | collective-permute-start | bytes 368648 | tf_op jit(solution)/shard_map/ppermute | solution.py:347
  21.7 27.2 %collective-permute-start.15 = (bf16[512,768]{1,0:T(8,128)(2,1)S(1)}, bf16[512,768]{1,0:T(8,128)(2,1)}, u32[]{:S(2)}, u32[]{:S(2)}) collective-permute-start(bf16[512,768]{1,0:T(8,128)(2,1)S(1)} %pad_maximum_fusion.5), channel_id=1, source_target_pairs={{0,1},{1,0},{2,3},{3,2},{4,5},{5,4},{6,7},{7,6},{8,9},{9,8},{10,11... | collective-permute-start | bytes 2359304 | tf_op jit(solution)/shard_map/ppermute | solution.py:347
  21.8 24.6 %copy-start.38 = (bf16[1,96,768]{2,1,0:T(8,128)(2,1)}, bf16[1,96,768]{2,1,0:T(8,128)(2,1)S(1)}, u32[]{:S(2)}) copy-start(bf16[1,96,768]{2,1,0:T(8,128)(2,1)S(1)} %collective-permute-done.6.refs_1_) | copy-start | bytes 442372
  21.8 24.6 %copy-start.39 = (bf16[1,96,768]{2,1,0:T(8,128)(2,1)}, bf16[1,96,768]{2,1,0:T(8,128)(2,1)S(1)}, u32[]{:S(2)}) copy-start(bf16[1,96,768]{2,1,0:T(8,128)(2,1)S(1)} %collective-permute-done.7.refs_2_) | copy-start | bytes 442372
  29.3 12.0 %collective-permute-start.8 = (bf16[4,48,1280]{2,1,0:T(8,128)(2,1)}, bf16[4,48,1280]{2,1,0:T(8,128)(2,1)}, u32[]{:S(2)}, u32[]{:S(2)}) collective-permute-start(bf16[4,48,1280]{2,1,0:T(8,128)(2,1)} %bitcast.184), channel_id=1, source_target_pairs={{0,2},{1,5},{2,0},{3,7},{4,6},{5,1},{6,4},{7,3},{8,10},{9,13},{10,... | collective-permute-start | bytes 1474568 | tf_op jit(solution)/shard_map/ppermute | solution.py:347
  29.8 11.4 %collective-permute-start.9 = (bf16[4,48,1280]{2,1,0:T(8,128)(2,1)}, bf16[4,48,1280]{2,1,0:T(8,128)(2,1)S(1)}, u32[]{:S(2)}, u32[]{:S(2)}) collective-permute-start(bf16[4,48,1280]{2,1,0:T(8,128)(2,1)} %bitcast.185), channel_id=1, source_target_pairs={{0,4},{1,3},{2,6},{3,1},{4,0},{5,7},{6,2},{7,5},{8,12},{9,11},{10,... | collective-permute-start | bytes 1474568 | tf_op jit(solution)/shard_map/ppermute | solution.py:347
  30.0 20.2 %copy-start.25 = (bf16[1,48,1920]{2,1,0:T(8,128)(2,1)}, bf16[1,48,1920]{2,1,0:T(8,128)(2,1)S(1)}, u32[]{:S(2)}) copy-start(bf16[1,48,1920]{2,1,0:T(8,128)(2,1)S(1)} %maximum_select_fusion.7.refs_0_) | copy-start | bytes 552964
  30.0 6.1 %collective-permute-start.10 = (bf16[1,48,1920]{2,1,0:T(8,128)(2,1)S(1)}, bf16[1,48,1920]{2,1,0:T(8,128)(2,1)S(1)}, u32[]{:S(2)}, u32[]{:S(2)}) collective-permute-start(bf16[1,48,1920]{2,1,0:T(8,128)(2,1)S(1)} %maximum_select_fusion.7.refs_0_), channel_id=1, source_target_pairs={{0,8},{1,17},{2,10},{3,19},{4,12},{5,21},{6,14},{7,23},{8,0},{9,25... | collective-permute-start | bytes 552968 | tf_op jit(solution)/shard_map/ppermute | solution.py:347
  31.2 8.9 %collective-permute-start.11 = (bf16[1,48,1920]{2,1,0:T(8,128)(2,1)S(1)}, bf16[1,48,1920]{2,1,0:T(8,128)(2,1)S(1)}, u32[]{:S(2)}, u32[]{:S(2)}) collective-permute-start(bf16[1,48,1920]{2,1,0:T(8,128)(2,1)S(1)} %maximum_select_fusion.7.refs_0_), channel_id=1, source_target_pairs={{0,16},{1,9},{2,18},{3,11},{4,20},{5,13},{6,22},{7,15},{8,24},{9,1... | collective-permute-start | bytes 552968 | tf_op jit(solution)/shard_map/ppermute | solution.py:347
  36.1 14.4 %copy-start.33 = (bf16[1,48,1920]{2,1,0:T(8,128)(2,1)}, bf16[1,48,1920]{2,1,0:T(8,128)(2,1)S(1)}, u32[]{:S(2)}) copy-start(bf16[1,48,1920]{2,1,0:T(8,128)(2,1)S(1)} %collective-permute-done.10.refs_1_) | copy-start | bytes 552964
  36.1 5.1 %collective-permute-start.12 = (bf16[1,96,768]{2,1,0:T(8,128)(2,1)S(1)}, bf16[1,96,768]{2,1,0:T(8,128)(2,1)S(1)}, u32[]{:S(2)}, u32[]{:S(2)}) collective-permute-start(bf16[1,96,768]{2,1,0:T(8,128)(2,1)S(1)} %collective-permute-done.6.refs_1_), channel_id=1, source_target_pairs={{0,4},{1,3},{2,6},{3,1},{4,0},{5,7},{6,2},{7,5},{8,12},{9,11},{10,... | collective-permute-start | bytes 442376 | tf_op jit(solution)/shard_map/ppermute | solution.py:347
  41.3 9.2 %collective-permute-start.13 = (bf16[4,48,1280]{2,1,0:T(8,128)(2,1)}, bf16[4,48,1280]{2,1,0:T(8,128)(2,1)}, u32[]{:S(2)}, u32[]{:S(2)}) collective-permute-start(bf16[4,48,1280]{2,1,0:T(8,128)(2,1)} %collective-permute-done.8.refs_1_), channel_id=1, source_target_pairs={{0,4},{1,3},{2,6},{3,1},{4,0},{5,7},{6,2},{7,5},{8,12},{9,11},{10,... | collective-permute-start | bytes 1474568 | tf_op jit(solution)/shard_map/ppermute | solution.py:347
  42.8 7.4 %collective-permute-start.14 = (bf16[1,48,1920]{2,1,0:T(8,128)(2,1)S(1)}, bf16[1,48,1920]{2,1,0:T(8,128)(2,1)}, u32[]{:S(2)}, u32[]{:S(2)}) collective-permute-start(bf16[1,48,1920]{2,1,0:T(8,128)(2,1)S(1)} %collective-permute-done.10.refs_1_), channel_id=1, source_target_pairs={{0,16},{1,9},{2,18},{3,11},{4,20},{5,13},{6,22},{7,15},{8,24},{9,1... | collective-permute-start | bytes 552968 | tf_op jit(solution)/shard_map/ppermute | solution.py:347
  50.2 15.9 %copy-start.13 = (bf16[1024,768]{1,0:T(8,128)(2,1)}, bf16[1024,768]{1,0:T(8,128)(2,1)S(1)}, u32[]{:S(2)}) copy-start(bf16[1024,768]{1,0:T(8,128)(2,1)S(1)} %pad_maximum_fusion) | copy-start | bytes 4718596
  53.1 13.0 %copy-start.71 = (f32[1152]{0:T(1024)S(1)}, f32[1152]{0:T(1024)}, u32[]{:S(2)}) copy-start(f32[1152]{0:T(1024)} %constant.169.clone.1) | copy-start | bytes 13828
  53.1 28.8 %collective-permute-start.16 = (bf16[4,48,1920]{2,1,0:T(8,128)(2,1)}, bf16[4,48,1920]{2,1,0:T(8,128)(2,1)}, u32[]{:S(2)}, u32[]{:S(2)}) collective-permute-start(bf16[4,48,1920]{2,1,0:T(8,128)(2,1)} %bitcast.172), channel_id=1, source_target_pairs={{0,2},{1,5},{2,0},{3,7},{4,6},{5,1},{6,4},{7,3},{8,10},{9,13},{10,... | collective-permute-start | bytes 2211848 | tf_op jit(solution)/shard_map/ppermute | solution.py:347
  54.6 27.3 %collective-permute-start.17 = (bf16[4,48,1920]{2,1,0:T(8,128)(2,1)}, bf16[4,48,1920]{2,1,0:T(8,128)(2,1)}, u32[]{:S(2)}, u32[]{:S(2)}) collective-permute-start(bf16[4,48,1920]{2,1,0:T(8,128)(2,1)} %bitcast.173), channel_id=1, source_target_pairs={{0,4},{1,3},{2,6},{3,1},{4,0},{5,7},{6,2},{7,5},{8,12},{9,11},{10,... | collective-permute-start | bytes 2211848 | tf_op jit(solution)/shard_map/ppermute | solution.py:347
  56.1 25.8 %collective-permute-start.18 = (bf16[1,384,768]{2,1,0:T(8,128)(2,1)S(1)}, bf16[1,384,768]{2,1,0:T(8,128)(2,1)}, u32[]{:S(2)}, u32[]{:S(2)}) collective-permute-start(bf16[1,384,768]{2,1,0:T(8,128)(2,1)S(1)} %bitcast.176), channel_id=1, source_target_pairs={{0,8},{1,17},{2,10},{3,19},{4,12},{5,21},{6,14},{7,23},{8,0},{9,25... | collective-permute-start | bytes 1769480 | tf_op jit(solution)/shard_map/ppermute | solution.py:347
  57.5 24.5 %collective-permute-start.19 = (bf16[1,384,768]{2,1,0:T(8,128)(2,1)S(1)}, bf16[1,384,768]{2,1,0:T(8,128)(2,1)}, u32[]{:S(2)}, u32[]{:S(2)}) collective-permute-start(bf16[1,384,768]{2,1,0:T(8,128)(2,1)S(1)} %bitcast.177), channel_id=1, source_target_pairs={{0,16},{1,9},{2,18},{3,11},{4,20},{5,13},{6,22},{7,15},{8,24},{9,1... | collective-permute-start | bytes 1769480 | tf_op jit(solution)/shard_map/ppermute | solution.py:347
  82.0 16.7 %collective-permute-start.21 = (bf16[4,48,1920]{2,1,0:T(8,128)(2,1)}, bf16[4,48,1920]{2,1,0:T(8,128)(2,1)S(1)}, u32[]{:S(2)}, u32[]{:S(2)}) collective-permute-start(bf16[4,48,1920]{2,1,0:T(8,128)(2,1)} %collective-permute-done.16.refs_1_), channel_id=1, source_target_pairs={{0,4},{1,3},{2,6},{3,1},{4,0},{5,7},{6,2},{7,5},{8,12},{9,11},{10,... | collective-permute-start | bytes 2211848 | tf_op jit(solution)/shard_map/ppermute | solution.py:347
  103.0 2.8 collective-permute-start.22
  103.2 2.7 collective-permute-start.20
  107.5 6.3 %collective-permute-start.24 = (bf16[512,768]{1,0:T(8,128)(2,1)S(1)}, bf16[512,768]{1,0:T(8,128)(2,1)}, u32[]{:S(2)}, u32[]{:S(2)}) collective-permute-start(bf16[512,768]{1,0:T(8,128)(2,1)S(1)} %fusion.21), channel_id=1, source_target_pairs={{0,1},{1,0},{2,3},{3,2},{4,5},{5,4},{6,7},{7,6},{8,9},{9,8},{10,11... | collective-permute-start | bytes 2359304 | tf_op jit(solution)/shard_map/ppermute | solution.py:347
  107.8 15.5 %collective-permute-start.23 = (bf16[1,384,768]{2,1,0:T(8,128)(2,1)}, bf16[1,384,768]{2,1,0:T(8,128)(2,1)}, u32[]{:S(2)}, u32[]{:S(2)}) collective-permute-start(bf16[1,384,768]{2,1,0:T(8,128)(2,1)} %collective-permute-done.18.refs_1_), channel_id=1, source_target_pairs={{0,16},{1,9},{2,18},{3,11},{4,20},{5,13},{6,22},{7,15},{8,24},{9,1... | collective-permute-start | bytes 1769480 | tf_op jit(solution)/shard_map/ppermute | solution.py:347
  111.4 9.9 %collective-permute-start.25 = (bf16[256,768]{1,0:T(8,128)(2,1)}, bf16[256,768]{1,0:T(8,128)(2,1)S(1)}, u32[]{:S(2)}, u32[]{:S(2)}) collective-permute-start(bf16[256,768]{1,0:T(8,128)(2,1)} %get-tuple-element.283), channel_id=1, source_target_pairs={{0,2},{1,3},{2,0},{3,1},{4,6},{5,7},{6,4},{7,5},{8,10},{9,11},{10,... | collective-permute-start | bytes 1179656 | tf_op jit(solution)/shard_map/ppermute | solution.py:347
  134.7 2.4 collective-permute-start.26
  141.3 2.3 collective-permute-start.28
  154.7 7.6 %collective-permute-start.29 = (bf16[512,768]{1,0:T(8,128)(2,1)}, bf16[512,768]{1,0:T(8,128)(2,1)}, u32[]{:S(2)}, u32[]{:S(2)}) collective-permute-start(bf16[512,768]{1,0:T(8,128)(2,1)} %slice.280), channel_id=1, source_target_pairs={{0,1},{1,0},{2,3},{3,2},{4,5},{5,4},{6,7},{7,6},{8,9},{9,8},{10,11... | collective-permute-start | bytes 2359304 | tf_op jit(solution)/shard_map/ppermute | solution.py:347
  171.0 14.7 %collective-permute-start.32 = (bf16[768,384]{1,0:T(8,128)(2,1)}, bf16[768,384]{1,0:T(8,128)(2,1)}, u32[]{:S(2)}, u32[]{:S(2)}) collective-permute-start(bf16[768,384]{1,0:T(8,128)(2,1)} %bitcast.51), channel_id=1, source_target_pairs={{0,1},{1,0},{2,3},{3,2},{4,5},{5,4},{6,7},{7,6},{8,9},{9,8},{10,11... | collective-permute-start | bytes 1769480 | tf_op jit(solution)/shard_map/ppermute | solution.py:347
  175.2 9.4 %collective-permute-start.33 = (bf16[512,384]{1,0:T(8,128)(2,1)S(1)}, bf16[512,384]{1,0:T(8,128)(2,1)S(1)}, u32[]{:S(2)}, u32[]{:S(2)}) collective-permute-start(bf16[512,384]{1,0:T(8,128)(2,1)S(1)} %bitcast.205), channel_id=1, source_target_pairs={{0,1},{1,0},{2,3},{3,2},{4,5},{5,4},{6,7},{7,6},{8,9},{9,8},{10,11... | collective-permute-start | bytes 1179656 | tf_op jit(solution)/shard_map/ppermute | solution.py:347
  181.3 47.4 %collective-permute-start.30 = (bf16[1,384,768]{2,1,0:T(8,128)(2,1)}, bf16[1,384,768]{2,1,0:T(8,128)(2,1)}, u32[]{:S(2)}, u32[]{:S(2)}) collective-permute-start(bf16[1,384,768]{2,1,0:T(8,128)(2,1)} %get-tuple-element.149), channel_id=1, source_target_pairs={{0,16},{1,9},{2,18},{3,11},{4,20},{5,13},{6,22},{7,15},{8,24},{9,1... | collective-permute-start | bytes 1769480 | tf_op jit(solution)/shard_map/ppermute | solution.py:347
  182.9 45.9 %collective-permute-start.31 = (bf16[1,384,768]{2,1,0:T(8,128)(2,1)}, bf16[1,384,768]{2,1,0:T(8,128)(2,1)}, u32[]{:S(2)}, u32[]{:S(2)}) collective-permute-start(bf16[1,384,768]{2,1,0:T(8,128)(2,1)} %get-tuple-element.150), channel_id=1, source_target_pairs={{0,16},{1,9},{2,18},{3,11},{4,20},{5,13},{6,22},{7,15},{8,24},{9,1... | collective-permute-start | bytes 1769480 | tf_op jit(solution)/shard_map/ppermute | solution.py:347
  191.3 37.4 %collective-permute-start.34 = (bf16[4,48,1920]{2,1,0:T(8,128)(2,1)}, bf16[4,48,1920]{2,1,0:T(8,128)(2,1)}, u32[]{:S(2)}, u32[]{:S(2)}) collective-permute-start(bf16[4,48,1920]{2,1,0:T(8,128)(2,1)} %get-tuple-element.155), channel_id=1, source_target_pairs={{0,4},{1,3},{2,6},{3,1},{4,0},{5,7},{6,2},{7,5},{8,12},{9,11},{10,... | collective-permute-start | bytes 2211848 | tf_op jit(solution)/shard_map/ppermute | solution.py:347
  191.4 37.3 %collective-permute-start.35 = (bf16[4,48,1920]{2,1,0:T(8,128)(2,1)}, bf16[4,48,1920]{2,1,0:T(8,128)(2,1)S(1)}, u32[]{:S(2)}, u32[]{:S(2)}) collective-permute-start(bf16[4,48,1920]{2,1,0:T(8,128)(2,1)} %get-tuple-element.156), channel_id=1, source_target_pairs={{0,4},{1,3},{2,6},{3,1},{4,0},{5,7},{6,2},{7,5},{8,12},{9,11},{10,... | collective-permute-start | bytes 2211848 | tf_op jit(solution)/shard_map/ppermute | solution.py:347
  193.5 12.5 %collective-permute-start.27 = (bf16[256,768]{1,0:T(8,128)(2,1)S(1)}, bf16[256,768]{1,0:T(8,128)(2,1)S(1)}, u32[]{:S(2)}, u32[]{:S(2)}) collective-permute-start(bf16[256,768]{1,0:T(8,128)(2,1)S(1)} %get-tuple-element.289), channel_id=1, source_target_pairs={{0,2},{1,3},{2,0},{3,1},{4,6},{5,7},{6,4},{7,5},{8,10},{9,11},{10,... | collective-permute-start | bytes 1179656 | tf_op jit(solution)/shard_map/ppermute | solution.py:347
  235.4 50.3 %collective-permute-start.36 = (bf16[512,768]{1,0:T(8,128)(2,1)}, bf16[512,768]{1,0:T(8,128)(2,1)S(1)}, u32[]{:S(2)}, u32[]{:S(2)}) collective-permute-start(bf16[512,768]{1,0:T(8,128)(2,1)} %slice.279), channel_id=1, source_target_pairs={{0,1},{1,0},{2,3},{3,2},{4,5},{5,4},{6,7},{7,6},{8,9},{9,8},{10,11... | collective-permute-start | bytes 2359304 | tf_op jit(solution)/shard_map/ppermute | solution.py:347
  251.2 16.5 %collective-permute-start.40 = (bf16[1,384,768]{2,1,0:T(8,128)(2,1)}, bf16[1,384,768]{2,1,0:T(8,128)(2,1)}, u32[]{:S(2)}, u32[]{:S(2)}) collective-permute-start(bf16[1,384,768]{2,1,0:T(8,128)(2,1)} %add_convert_fusion.4), channel_id=1, source_target_pairs={{0,8},{1,17},{2,10},{3,19},{4,12},{5,21},{6,14},{7,23},{8,0},{9,25... | collective-permute-start | bytes 1769480 | tf_op jit(solution)/shard_map/ppermute | solution.py:347
  253.6 14.1 %collective-permute-start.41 = (bf16[4,48,1920]{2,1,0:T(8,128)(2,1)}, bf16[4,48,1920]{2,1,0:T(8,128)(2,1)}, u32[]{:S(2)}, u32[]{:S(2)}) collective-permute-start(bf16[4,48,1920]{2,1,0:T(8,128)(2,1)} %add_convert_fusion.2), channel_id=1, source_target_pairs={{0,2},{1,5},{2,0},{3,7},{4,6},{5,1},{6,4},{7,3},{8,10},{9,13},{10,... | collective-permute-start | bytes 2211848 | tf_op jit(solution)/shard_map/ppermute | solution.py:347
  262.8 15.0 %collective-permute-start.38 = (bf16[4,48,1280]{2,1,0:T(8,128)(2,1)}, bf16[4,48,1280]{2,1,0:T(8,128)(2,1)}, u32[]{:S(2)}, u32[]{:S(2)}) collective-permute-start(bf16[4,48,1280]{2,1,0:T(8,128)(2,1)} %get-tuple-element.161), channel_id=1, source_target_pairs={{0,4},{1,3},{2,6},{3,1},{4,0},{5,7},{6,2},{7,5},{8,12},{9,11},{10,... | collective-permute-start | bytes 1474568 | tf_op jit(solution)/shard_map/ppermute | solution.py:347
  266.0 12.4 %collective-permute-start.39 = (bf16[4,48,1280]{2,1,0:T(8,128)(2,1)}, bf16[4,48,1280]{2,1,0:T(8,128)(2,1)}, u32[]{:S(2)}, u32[]{:S(2)}) collective-permute-start(bf16[4,48,1280]{2,1,0:T(8,128)(2,1)} %get-tuple-element.162), channel_id=1, source_target_pairs={{0,4},{1,3},{2,6},{3,1},{4,0},{5,7},{6,2},{7,5},{8,12},{9,11},{10,... | collective-permute-start | bytes 1474568 | tf_op jit(solution)/shard_map/ppermute | solution.py:347
  272.4 13.4 %copy-start.4 = (f32[512,768]{1,0:T(8,128)S(1)}, f32[512,768]{1,0:T(8,128)}, u32[]{:S(2)}) copy-start(f32[512,768]{1,0:T(8,128)} %copy-done.3) | copy-start | bytes 4718596
  279.7 19.5 %collective-permute-start.42 = (bf16[4,48,1280]{2,1,0:T(8,128)(2,1)S(1)}, bf16[4,48,1280]{2,1,0:T(8,128)(2,1)S(1)}, u32[]{:S(2)}, u32[]{:S(2)}) collective-permute-start(bf16[4,48,1280]{2,1,0:T(8,128)(2,1)S(1)} %add_convert_fusion.6), channel_id=1, source_target_pairs={{0,2},{1,5},{2,0},{3,7},{4,6},{5,1},{6,4},{7,3},{8,10},{9,13},{10,... | collective-permute-start | bytes 1474568 | tf_op jit(solution)/shard_map/ppermute | solution.py:347
  280.2 7.5 %collective-permute-start.43 = (bf16[1,96,768]{2,1,0:T(8,128)(2,1)}, bf16[1,96,768]{2,1,0:T(8,128)(2,1)S(1)}, u32[]{:S(2)}, u32[]{:S(2)}) collective-permute-start(bf16[1,96,768]{2,1,0:T(8,128)(2,1)} %get-tuple-element.184), channel_id=1, source_target_pairs={{0,4},{1,3},{2,6},{3,1},{4,0},{5,7},{6,2},{7,5},{8,12},{9,11},{10,... | collective-permute-start | bytes 442376 | tf_op jit(solution)/shard_map/ppermute | solution.py:347
  282.8 7.1 %collective-permute-start.44 = (bf16[1,96,768]{2,1,0:T(8,128)(2,1)S(1)}, bf16[1,96,768]{2,1,0:T(8,128)(2,1)S(1)}, u32[]{:S(2)}, u32[]{:S(2)}) collective-permute-start(bf16[1,96,768]{2,1,0:T(8,128)(2,1)S(1)} %copy-done.70), channel_id=1, source_target_pairs={{0,4},{1,3},{2,6},{3,1},{4,0},{5,7},{6,2},{7,5},{8,12},{9,11},{10,... | collective-permute-start | bytes 442376 | tf_op jit(solution)/shard_map/ppermute | solution.py:347
  282.8 8.5 %collective-permute-start.45 = (bf16[1,48,1920]{2,1,0:T(8,128)(2,1)}, bf16[1,48,1920]{2,1,0:T(8,128)(2,1)S(1)}, u32[]{:S(2)}, u32[]{:S(2)}) collective-permute-start(bf16[1,48,1920]{2,1,0:T(8,128)(2,1)} %get-tuple-element.186), channel_id=1, source_target_pairs={{0,16},{1,9},{2,18},{3,11},{4,20},{5,13},{6,22},{7,15},{8,24},{9,1... | collective-permute-start | bytes 552968 | tf_op jit(solution)/shard_map/ppermute | solution.py:347
  285.7 13.4 %collective-permute-start.46 = (bf16[1,48,1920]{2,1,0:T(8,128)(2,1)}, bf16[1,48,1920]{2,1,0:T(8,128)(2,1)S(1)}, u32[]{:S(2)}, u32[]{:S(2)}) collective-permute-start(bf16[1,48,1920]{2,1,0:T(8,128)(2,1)} %get-tuple-element.187), channel_id=1, source_target_pairs={{0,16},{1,9},{2,18},{3,11},{4,20},{5,13},{6,22},{7,15},{8,24},{9,1... | collective-permute-start | bytes 552968 | tf_op jit(solution)/shard_map/ppermute | solution.py:347
  287.7 14.3 %collective-permute-start.37 = (bf16[256,768]{1,0:T(8,128)(2,1)S(1)}, bf16[256,768]{1,0:T(8,128)(2,1)S(1)}, u32[]{:S(2)}, u32[]{:S(2)}) collective-permute-start(bf16[256,768]{1,0:T(8,128)(2,1)S(1)} %get-tuple-element.285), channel_id=1, source_target_pairs={{0,2},{1,3},{2,0},{3,1},{4,6},{5,7},{6,4},{7,5},{8,10},{9,11},{10,... | collective-permute-start | bytes 1179656 | tf_op jit(solution)/shard_map/ppermute | solution.py:347
  299.2 6.4 %collective-permute-start.47 = (bf16[1,96,768]{2,1,0:T(8,128)(2,1)S(1)}, bf16[1,96,768]{2,1,0:T(8,128)(2,1)S(1)}, u32[]{:S(2)}, u32[]{:S(2)}) collective-permute-start(bf16[1,96,768]{2,1,0:T(8,128)(2,1)S(1)} %add_convert_fusion.8), channel_id=1, source_target_pairs={{0,2},{1,5},{2,0},{3,7},{4,6},{5,1},{6,4},{7,3},{8,10},{9,13},{10,... | collective-permute-start | bytes 442376 | tf_op jit(solution)/shard_map/ppermute | solution.py:347
  299.3 6.7 %collective-permute-start.48 = (bf16[1,48,1920]{2,1,0:T(8,128)(2,1)S(1)}, bf16[1,48,1920]{2,1,0:T(8,128)(2,1)S(1)}, u32[]{:S(2)}, u32[]{:S(2)}) collective-permute-start(bf16[1,48,1920]{2,1,0:T(8,128)(2,1)S(1)} %add_convert_fusion.7), channel_id=1, source_target_pairs={{0,8},{1,17},{2,10},{3,19},{4,12},{5,21},{6,14},{7,23},{8,0},{9,25... | collective-permute-start | bytes 552968 | tf_op jit(solution)/shard_map/ppermute | solution.py:347
  306.0 7.3 %collective-permute-start.49 = (bf16[1,48,1280]{2,1,0:T(8,128)(2,1)}, bf16[1,48,1280]{2,1,0:T(8,128)(2,1)S(1)}, u32[]{:S(2)}, u32[]{:S(2)}) collective-permute-start(bf16[1,48,1280]{2,1,0:T(8,128)(2,1)} %get-tuple-element.198), channel_id=1, source_target_pairs={{0,16},{1,9},{2,18},{3,11},{4,20},{5,13},{6,22},{7,15},{8,24},{9,1... | collective-permute-start | bytes 368648 | tf_op jit(solution)/shard_map/ppermute | solution.py:347
  308.9 9.5 %collective-permute-start.50 = (bf16[1,48,1280]{2,1,0:T(8,128)(2,1)}, bf16[1,48,1280]{2,1,0:T(8,128)(2,1)S(1)}, u32[]{:S(2)}, u32[]{:S(2)}) collective-permute-start(bf16[1,48,1280]{2,1,0:T(8,128)(2,1)} %get-tuple-element.199), channel_id=1, source_target_pairs={{0,16},{1,9},{2,18},{3,11},{4,20},{5,13},{6,22},{7,15},{8,24},{9,1... | collective-permute-start | bytes 368648 | tf_op jit(solution)/shard_map/ppermute | solution.py:347
  309.1 1.4 collective-permute-start.53
  310.0 13.4 %copy-start.42 = (bf16[1,48,1280]{2,1,0:T(8,128)(2,1)S(1)}, bf16[1,48,1280]{2,1,0:T(8,128)(2,1)}, u32[]{:S(2)}) copy-start(bf16[1,48,1280]{2,1,0:T(8,128)(2,1)} %get-tuple-element.197) | copy-start | bytes 368644
  318.5 4.9 %collective-permute-start.51 = (bf16[1,48,1280]{2,1,0:T(8,128)(2,1)S(1)}, bf16[1,48,1280]{2,1,0:T(8,128)(2,1)S(1)}, u32[]{:S(2)}, u32[]{:S(2)}) collective-permute-start(bf16[1,48,1280]{2,1,0:T(8,128)(2,1)S(1)} %add_convert_fusion.9), channel_id=1, source_target_pairs={{0,8},{1,17},{2,10},{3,19},{4,12},{5,21},{6,14},{7,23},{8,0},{9,25... | collective-permute-start | bytes 368648 | tf_op jit(solution)/shard_map/ppermute | solution.py:347
  323.5 1.3 collective-permute-start.52
  (63 other events, 314.6 us)
